TPU v7x, 32 devices: a whole 2x2x4 slice. The times are simulated.
32 devices in a mesh: loop: 4 (over x, core), grp: 8 (over z, y).
Axes of the slice: x: 2, y: 2, z: 4, core: 2. Of those that a mesh axis runs over, the one named last changes fastest.
Arguments:
- basis: bfloat16 [24576, 256], P(('loop', 'grp')), may hold values from -6 to 6
- stiffness: bfloat16 [384, 16, 4096], P(('loop', 'grp')), may hold values from -0.1875 to 0.1875
- mass: bfloat16 [384, 16, 4096], P(('loop', 'grp')), may hold values from -0.1875 to 0.1875
- col_index: int32 [384, 16], P(('loop', 'grp')), may hold values from 0 to 11
- live_counts: int32 [384], P(('loop', 'grp')), may hold values from 1 to 16, as said below
Outputs:
- stiff_basis: bfloat16 [24576, 256], P(('loop', 'grp'))
- mass_basis: bfloat16 [24576, 256], P(('loop', 'grp'))
- stiff_gram: float32 [256, 256], replicated
- mass_gram: float32 [256, 256], replicated
Inputs may be any that keep to these rules, and one draw needn't show every extreme that they name: `live_counts`: every block row keeps at least one block; some block row uses all 16 and some only one.
All inputs are finite; a program needn't handle non-finite values.
Results may differ from a plain program's by a relative error of at most 0.0029.
Values may be sent and summed in bfloat16 or wider, within the bound.
A program may use at most 64 MiB of HBM per device.

v0:
```python
import jax
import jax.numpy as jnp
from jax import lax
from jax.sharding import PartitionSpec as P

BS = 64
NB = 16


panel_spans = ((0, 0, 6), (1, 6, 3), (-1, 9, 3), (2, 12, 2), (-2, 14, 2))


def shifted(block, axis, distance):
    devices = range(lax.axis_size(axis))
    route = [((i - distance) % len(devices), i) for i in devices]
    return lax.ppermute(block, axis, route)


def on_device(basis, stiffness, mass, col_index, live_counts):
    rows_dev = stiffness.shape[0]
    width = basis.shape[1]
    kb = stiffness.reshape(rows_dev, NB, BS, BS)
    mb = mass.reshape(rows_dev, NB, BS, BS)
    slot_ids = jnp.arange(NB, dtype=jnp.int32)
    live_grid = slot_ids[None, :] < live_counts[:, None]
    panels = {
        0: basis,
        1: shifted(basis, "loop", -1),
        -1: shifted(basis, "loop", 1),
        2: shifted(basis, "loop", -2),
        -2: shifted(basis, "loop", 2),
    }
    zeros_acc = jnp.zeros((rows_dev, BS, width), jnp.float32)
    accs = (zeros_acc, zeros_acc)
    for shift_by, first, count in panel_spans:
        blocks = panels[shift_by].reshape(rows_dev, BS, width)
        chosen = col_index[:, first : first + count]
        alive = live_grid[:, first : first + count]
        picked = blocks[chosen]
        picked = jnp.where(alive[:, :, None, None], picked, jnp.zeros_like(picked))
        kadd = jnp.einsum(
            "rjab,rjbc->rac",
            kb[:, first : first + count],
            picked,
            preferred_element_type=jnp.float32,
        )
        madd = jnp.einsum(
            "rjab,rjbc->rac",
            mb[:, first : first + count],
            picked,
            preferred_element_type=jnp.float32,
        )
        accs = (accs[0] + kadd, accs[1] + madd)
    kacc, macc = accs
    stiff_basis = kacc.reshape(rows_dev * BS, width).astype(jnp.bfloat16)
    mass_basis = macc.reshape(rows_dev * BS, width).astype(jnp.bfloat16)
    contract = (((0,), (0,)), ((), ()))
    kterm = lax.dot_general(basis, stiff_basis, contract, preferred_element_type=jnp.float32)
    mterm = lax.dot_general(basis, mass_basis, contract, preferred_element_type=jnp.float32)
    kgram, mgram = lax.psum((kterm, mterm), ("loop", "grp"))
    total_dofs = basis.shape[0] * lax.axis_size("loop") * lax.axis_size("grp")
    factor = jnp.float32(1.0) / jnp.sqrt(jnp.float32(total_dofs))
    return (stiff_basis, mass_basis, kgram * factor, mgram * factor)


def solution(mesh):
    in_specs = (
        P(("loop", "grp"), None),
        P(("loop", "grp"), None, None),
        P(("loop", "grp"), None, None),
        P(("loop", "grp"), None),
        P(("loop", "grp")),
    )
    out_specs = (P(("loop", "grp"), None), P(("loop", "grp"), None), P(), P())
    return jax.shard_map(
        on_device, mesh=mesh, in_specs=in_specs, out_specs=out_specs, check_vma=False
    )
```

profile of v0, /device:TPU:0, one launch (start us, length us, event | category | flops | bytes accessed | tf_op | source)
XLA Modules:
  0.0 197.9 jit_solution(3938690956162846545)
XLA Ops:
  7.7 2.0 %collective-permute-start = (bf16[768,256]{1,0:T(8,128)(2,1)}, bf16[768,256]{1,0:T(8,128)(2,1)}, u32[]{:S(2)}, u32[]{:S(2)}) collective-permute-start(bf16[768,256]{1,0:T(8,128)(2,1)} %param.5), channel_id=1, source_target_pairs={{8,0},{16,8},{24,16},{0,24},{9,1},{17,9},{25,17},{1,25},{10,2},{18... | collective-permute-start | bytes 1179656 | tf_op jit(solution)/shard_map/ppermute | solution.py:16
  9.7 2.2 %collective-permute-start.2 = (bf16[768,256]{1,0:T(8,128)(2,1)}, bf16[768,256]{1,0:T(8,128)(2,1)}, u32[]{:S(2)}, u32[]{:S(2)}) collective-permute-start(bf16[768,256]{1,0:T(8,128)(2,1)} %param.5), channel_id=1, source_target_pairs={{16,0},{24,8},{0,16},{8,24},{17,1},{25,9},{1,17},{9,25},{18,2},{26... | collective-permute-start | bytes 1179656 | tf_op jit(solution)/shard_map/ppermute | solution.py:16
  11.9 0.8 compare_select_fusion.3
  15.5 0.8 compare_select_fusion.1
  16.4 4.3 %reshape.42 = bf16[12,16,64,64]{3,2,1,0:T(8,128)(2,1)S(1)} reshape(bf16[12,16,4096]{2,1,0:T(8,128)(2,1)} %param.7) | data formatting | bytes 3145728 | tf_op jit(solution)/shard_map/reshape | solution.py:23
  22.4 5.5 %reshape.38 = bf16[12,16,64,64]{3,2,1,0:T(8,128)(2,1)} reshape(bf16[12,16,4096]{2,1,0:T(8,128)(2,1)} %param.6) | data formatting | bytes 3145728 | tf_op jit(solution)/shard_map/reshape | solution.py:22
  27.9 2.4 %gather_fusion = bf16[72,64,256]{2,1,0:T(8,128)(2,1)} fusion(bf16[12,64,256]{2,1,0:T(8,128)(2,1)S(1)} %bitcast.84, s32[1024]{0:T(1024)S(1)} %pad_clamp_fusion.4), kind=kCustom, calls=%fused_computation | custom fusion | bytes 4718880 | tf_op jit(solution)/shard_map/gather | solution.py:39
  30.3 3.3 %fusion.2 = f32[12,256,64]{1,2,0:T(8,128)} fusion(bf16[12,16,64,64]{3,2,1,0:T(8,128)(2,1)S(1)} %reshape.42, bf16[12,6,64,256]{3,2,1,0:T(8,128)(2,1)} %bitcast.91, pred[12,6]{1,0:T(8,128)(4,1)S(1)} %bitcast.99), kind=kOutput, calls=%fused_computation.8 | convolution fusion | flops 152174592 | bytes 4718664 | tf_op jit(solution)/shard_map/rjab,rjbc->rac/dot_general | solution.py:47
  33.6 1.5 fusion.3
  35.2 2.6 %gather_fusion.4 = bf16[24,64,256]{2,1,0:T(8,128)(2,1)} fusion(bf16[12,64,256]{2,1,0:T(8,128)(2,1)} %bitcast.12, s32[1024]{0:T(1024)S(1)} %copy-done.15), kind=kCustom, calls=%fused_computation.4 | custom fusion | bytes 1572960 | tf_op jit(solution)/shard_map/gather | solution.py:39
  37.7 2.6 %gather_fusion.3 = bf16[24,64,256]{2,1,0:T(8,128)(2,1)} fusion(bf16[12,64,256]{2,1,0:T(8,128)(2,1)} %bitcast.12, s32[1024]{0:T(1024)} %pad_clamp_fusion.1), kind=kCustom, calls=%fused_computation.3 | custom fusion | bytes 1572960 | tf_op jit(solution)/shard_map/gather | solution.py:39
  40.4 2.7 %gather_fusion.2 = bf16[36,64,256]{2,1,0:T(8,128)(2,1)} fusion(bf16[12,64,256]{2,1,0:T(8,128)(2,1)} %bitcast.8, s32[1024]{0:T(1024)S(1)} %pad_clamp_fusion.2), kind=kCustom, calls=%fused_computation.2 | custom fusion | bytes 2359440 | tf_op jit(solution)/shard_map/gather | solution.py:39
  43.1 2.7 %convolution_bitcast_fusion.4 = f32[12,256,64]{1,2,0:T(8,128)} fusion(bf16[12,16,64,64]{3,2,1,0:T(8,128)(2,1)S(1)} %reshape.42, bf16[12,3,64,256]{3,2,1,0:T(8,128)(2,1)} %bitcast.97, pred[12,3]{1,0:T(8,128)(4,1)S(1)} %copy-done.19), kind=kOutput, calls=%fused_computation.14 | convolution fusion | flops 76087296 | bytes 3538980 | tf_op jit(solution)/shard_map/rjab,rjbc->rac/dot_general | solution.py:47
  45.8 1.3 convolution_bitcast_fusion
  47.1 1.2 convolution_bitcast_fusion.2
  48.3 1.3 convolution_bitcast_fusion.6
  49.6 2.7 %gather_fusion.1 = bf16[36,64,256]{2,1,0:T(8,128)(2,1)} fusion(bf16[12,64,256]{2,1,0:T(8,128)(2,1)} %bitcast.4, s32[1024]{0:T(1024)S(1)} %pad_clamp_fusion.3), kind=kCustom, calls=%fused_computation.1 | custom fusion | bytes 2359440 | tf_op jit(solution)/shard_map/gather | solution.py:39
  52.4 2.3 %fusion.11 = f32[12,256,64]{1,2,0:T(8,128)S(1)} fusion(f32[12,256,64]{1,2,0:T(8,128)} %convolution_bitcast_fusion.4, f32[12,256,64]{1,2,0:T(8,128)} %fusion.2, bf16[12,16,64,64]{3,2,1,0:T(8,128)(2,1)S(1)} %reshape.42, bf16[12,3,64,256]{3,2,1,0:T(8,128)(2,1)} %bitcast.85, pred[12,3]{1,0:T(8,128)(4,1)S(1)} %copy-done.17), kind=kOutput, calls=%fused_computation.25 | convolution fusion | flops 76480512 | bytes 5111844 | tf_op jit(solution)/shard_map/rjab,rjbc->rac/dot_general | solution.py:47
  55.1 1.0 convolution_bitcast_fusion.8
  58.7 1.0 convolution_bitcast_fusion.9
  59.7 128.6 %all-reduce.3.cloned.1.call-done = (f32[256,256]{0,1:T(8,128)}, f32[256,256]{0,1:T(8,128)}) async-done(((f32[256,256]{0,1:T(8,128)}, f32[256,256]{0,1:T(8,128)}), (f32[256,256]{0,1:T(8,128)}, f32[256,256]{0,1:T(8,128)})) %all-reduce.3.cloned.1.call-update) | async-done | bytes 524304 | tf_op jit(solution)/shard_map/psum | solution.py:60
  188.3 1.1 broadcast_multiply_fusion
  189.4 0.8 copy.11
  190.2 0.8 copy.12
  (63 shorter events, 7.9 us)
Async XLA Ops:
  7.2 181.1 %all-reduce.3.cloned.1.call-start = ((), (), s32[]{:S(2)}) async-start(), calls=%async_computation | async-start | bytes 1048576 | tf_op jit(solution)/shard_map/psum | solution.py:60
  7.2 33.1 %collective-permute-start.1 = (bf16[768,256]{1,0:T(8,128)(2,1)}, bf16[768,256]{1,0:T(8,128)(2,1)}, u32[]{:S(2)}, u32[]{:S(2)}) collective-permute-start(bf16[768,256]{1,0:T(8,128)(2,1)} %param.5), channel_id=1, source_target_pairs={{24,0},{0,8},{8,16},{16,24},{25,1},{1,9},{9,17},{17,25},{26,2},{2,... | collective-permute-start | bytes 1179656 | tf_op jit(solution)/shard_map/ppermute | solution.py:16
  7.7 41.9 %collective-permute-start = (bf16[768,256]{1,0:T(8,128)(2,1)}, bf16[768,256]{1,0:T(8,128)(2,1)}, u32[]{:S(2)}, u32[]{:S(2)}) collective-permute-start(bf16[768,256]{1,0:T(8,128)(2,1)} %param.5), channel_id=1, source_target_pairs={{8,0},{16,8},{24,16},{0,24},{9,1},{17,9},{25,17},{1,25},{10,2},{18... | collective-permute-start | bytes 1179656 | tf_op jit(solution)/shard_map/ppermute | solution.py:16
  9.7 25.5 %collective-permute-start.2 = (bf16[768,256]{1,0:T(8,128)(2,1)}, bf16[768,256]{1,0:T(8,128)(2,1)}, u32[]{:S(2)}, u32[]{:S(2)}) collective-permute-start(bf16[768,256]{1,0:T(8,128)(2,1)} %param.5), channel_id=1, source_target_pairs={{16,0},{24,8},{0,16},{8,24},{17,1},{25,9},{1,17},{9,25},{18,2},{26... | collective-permute-start | bytes 1179656 | tf_op jit(solution)/shard_map/ppermute | solution.py:16
  22.4 5.5 %copy-start = (bf16[768,256]{1,0:T(8,128)(2,1)S(1)}, bf16[768,256]{1,0:T(8,128)(2,1)}, u32[]{:S(2)}) copy-start(bf16[768,256]{1,0:T(8,128)(2,1)} %param.5) | copy-start | bytes 1179652
  30.3 3.3 %copy-start.1 = (bf16[12,16,64,64]{3,2,1,0:T(8,128)(2,1)S(1)}, bf16[12,16,64,64]{3,2,1,0:T(8,128)(2,1)}, u32[]{:S(2)}) copy-start(bf16[12,16,64,64]{3,2,1,0:T(8,128)(2,1)} %reshape.38) | copy-start | bytes 4718596
  30.3 3.3 %copy-start.9 = (bf16[72,64,256]{2,1,0:T(8,128)(2,1)S(1)}, bf16[72,64,256]{2,1,0:T(8,128)(2,1)}, u32[]{:S(2)}) copy-start(bf16[72,64,256]{2,1,0:T(8,128)(2,1)} %gather_fusion) | copy-start | bytes 7077892
  33.6 1.5 copy-start.15
  37.7 5.4 %copy-start.19 = (pred[12,3]{1,0:T(8,128)(4,1)S(1)}, pred[12,3]{1,0:T(8,128)(4,1)}, u32[]{:S(2)}) copy-start(pred[12,3]{1,0:T(8,128)(4,1)} %get-tuple-element.21) | copy-start | bytes 112
  40.4 5.5 %copy-start.18 = (pred[12,2]{1,0:T(8,128)(4,1)S(1)}, pred[12,2]{1,0:T(8,128)(4,1)}, u32[]{:S(2)}) copy-start(pred[12,2]{1,0:T(8,128)(4,1)} %get-tuple-element.19) | copy-start | bytes 76
  43.1 2.7 %copy-start.6 = (bf16[24,64,256]{2,1,0:T(8,128)(2,1)S(1)}, bf16[24,64,256]{2,1,0:T(8,128)(2,1)}, u32[]{:S(2)}) copy-start(bf16[24,64,256]{2,1,0:T(8,128)(2,1)} %gather_fusion.4) | copy-start | bytes 2359300
  43.1 4.0 %copy-start.2 = (bf16[12,16,64,64]{3,2,1,0:T(8,128)(2,1)S(1)}, bf16[12,16,64,64]{3,2,1,0:T(8,128)(2,1)}, u32[]{:S(2)}) copy-start(bf16[12,16,64,64]{3,2,1,0:T(8,128)(2,1)} %reshape.38) | copy-start | bytes 4718596
  45.8 2.5 %copy-start.12 = (bf16[36,64,256]{2,1,0:T(8,128)(2,1)S(1)}, bf16[36,64,256]{2,1,0:T(8,128)(2,1)}, u32[]{:S(2)}) copy-start(bf16[36,64,256]{2,1,0:T(8,128)(2,1)} %gather_fusion.2) | copy-start | bytes 3538948
  48.3 4.0 %copy-start.17 = (pred[12,3]{1,0:T(8,128)(4,1)S(1)}, pred[12,3]{1,0:T(8,128)(4,1)}, u32[]{:S(2)}) copy-start(pred[12,3]{1,0:T(8,128)(4,1)} %get-tuple-element.20) | copy-start | bytes 112
  52.4 2.3 %copy-start.5 = (bf16[24,64,256]{2,1,0:T(8,128)(2,1)S(1)}, bf16[24,64,256]{2,1,0:T(8,128)(2,1)}, u32[]{:S(2)}) copy-start(bf16[24,64,256]{2,1,0:T(8,128)(2,1)} %gather_fusion.3) | copy-start | bytes 2359300
  52.4 2.3 %copy-start.8 = (f32[12,256,64]{1,2,0:T(8,128)S(1)}, f32[12,256,64]{1,2,0:T(8,128)}, u32[]{:S(2)}) copy-start(f32[12,256,64]{1,2,0:T(8,128)} %convolution_bitcast_fusion) | copy-start | bytes 2359300
  52.4 2.4 %copy-start.16 = (pred[12,2]{1,0:T(8,128)(4,1)S(1)}, pred[12,2]{1,0:T(8,128)(4,1)}, u32[]{:S(2)}) copy-start(pred[12,2]{1,0:T(8,128)(4,1)} %get-tuple-element.18) | copy-start | bytes 76
  52.4 3.7 %copy-start.13 = (f32[12,256,64]{1,2,0:T(8,128)S(1)}, f32[12,256,64]{1,2,0:T(8,128)}, u32[]{:S(2)}) copy-start(f32[12,256,64]{1,2,0:T(8,128)} %fusion.3) | copy-start | bytes 2359300
  52.4 3.7 %copy-start.14 = (f32[12,256,64]{1,2,0:T(8,128)S(1)}, f32[12,256,64]{1,2,0:T(8,128)}, u32[]{:S(2)}) copy-start(f32[12,256,64]{1,2,0:T(8,128)} %convolution_bitcast_fusion.6) | copy-start | bytes 2359300
  54.7 2.2 %copy-start.3 = (bf16[12,16,64,64]{3,2,1,0:T(8,128)(2,1)S(1)}, bf16[12,16,64,64]{3,2,1,0:T(8,128)(2,1)}, u32[]{:S(2)}) copy-start(bf16[12,16,64,64]{3,2,1,0:T(8,128)(2,1)} %reshape.38) | copy-start | bytes 4718596
  54.7 2.5 %copy-start.4 = (bf16[36,64,256]{2,1,0:T(8,128)(2,1)S(1)}, bf16[36,64,256]{2,1,0:T(8,128)(2,1)}, u32[]{:S(2)}) copy-start(bf16[36,64,256]{2,1,0:T(8,128)(2,1)} %gather_fusion.1) | copy-start | bytes 3538948
  55.1 2.6 %copy-start.10 = (bf16[12,256,64]{1,2,0:T(8,128)(2,1)}, bf16[12,256,64]{1,2,0:T(8,128)(2,1)S(1)}, u32[]{:S(2)}) copy-start(bf16[12,256,64]{1,2,0:T(8,128)(2,1)S(1)} %fusion.12) | copy-start | bytes 1179652
  57.2 1.1 copy-start.7
  58.7 132.4 %copy-start.11 = (bf16[12,256,64]{1,2,0:T(8,128)(2,1)}, bf16[12,256,64]{1,2,0:T(8,128)(2,1)S(1)}, u32[]{:S(2)}) copy-start(bf16[12,256,64]{1,2,0:T(8,128)(2,1)S(1)} %fusion.13) | copy-start | bytes 1179652
Sparse Core Ops, SparseCore 0:
  59.8 128.3 all-reduce.2
where the time goes:
time: 198 us
  waiting for transfers between devices  129 us (65%)
  local copies, waits for them, and re-layouts  28.2 us (14%)
  matrix products  16.7 us (8%)
  between operations  14.2 us (7%)
  other arithmetic  5.42 us (3%)
  starting transfers between devices  4.77 us (2%)
    psum x1, waiting for transfers between devices, on_device(): kgram, mgram = lax.psum((kterm, mterm), ('loop', 'grp'))  129 us
    gather x5, local copies, waits for them, and re-layouts, on_device(): picked = blocks[chosen]  13 us
    dot_general x5, matrix products, on_device(): jnp.einsum('rjab,rjbc->rac', mb[:, first:first + count], picked, preferre...  9.93 us
    reshape x1, local copies, waits for them, and re-layouts, on_device(): kb = stiffness.reshape(rows_dev, NB, BS, BS)  5.54 us
    dot_general x5, matrix products, on_device(): jnp.einsum('rjab,rjbc->rac', kb[:, first:first + count], picked, preferre...  4.76 us
    ppermute x3, starting transfers between devices, shifted(): return lax.ppermute(block, axis, route)  4.74 us
    reshape x1, local copies, waits for them, and re-layouts, on_device(): mb = mass.reshape(rows_dev, NB, BS, BS)  4.31 us
  transfers between devices with their start and end apart: 4, of which 1 were waited for; matrix products, arithmetic and copies ran while one was open for 19% of the time, Pallas kernels for 0%

commit v1 on v0

--- a/solution.py
+++ b/solution.py
@@ -1,6 +1,10 @@
+import functools
+
 import jax
 import jax.numpy as jnp
 from jax import lax
+from jax.experimental import pallas as pl
+from jax.experimental.pallas import tpu as pltpu
 from jax.sharding import PartitionSpec as P
 
 BS = 64
@@ -14,6 +18,107 @@
     devices = range(lax.axis_size(axis))
     route = [((i - distance) % len(devices), i) for i in devices]
     return lax.ppermute(block, axis, route)
+
+
+MESH = pl.DeviceIdType.MESH
+
+
+def greet(nl, ng):
+    me_l, me_g = lax.axis_index("loop"), lax.axis_index("grp")
+    barrier = pltpu.get_barrier_semaphore()
+    for d in range(1, nl):
+        pl.semaphore_signal(barrier, inc=1, device_id=(lax.rem(me_l + d, nl), me_g), device_id_type=MESH)
+    for d in range(1, ng):
+        pl.semaphore_signal(barrier, inc=1, device_id=(me_l, lax.rem(me_g + d, ng)), device_id_type=MESH)
+    pl.semaphore_wait(barrier, nl + ng - 2)
+
+
+def reduce_all(nl, ng, split, factor, part, land_l, red, land_g, res, sems):
+    me_l, me_g = lax.axis_index("loop"), lax.axis_index("grp")
+    send_a, recv_a, send_b, recv_b, send_c, recv_c, send_d, recv_d = sems
+
+    def to_loop(src, dst, send, recv, d):
+        return pltpu.make_async_remote_copy(
+            src_ref=src, dst_ref=dst, send_sem=send.at[d - 1], recv_sem=recv.at[d - 1],
+            device_id=(lax.rem(me_l + d, nl), me_g), device_id_type=MESH)
+
+    def to_grp(src, dst, send, recv, d):
+        return pltpu.make_async_remote_copy(
+            src_ref=src, dst_ref=dst, send_sem=send.at[d - 1], recv_sem=recv.at[d - 1],
+            device_id=(me_l, lax.rem(me_g + d, ng)), device_id_type=MESH)
+
+    copies = [to_loop(part.at[lax.rem(me_l + d, nl)], land_l.at[d - 1], send_a, recv_a, d) for d in range(1, nl)]
+    for c in copies:
+        c.start()
+    for c in copies:
+        c.wait()
+    total = part[me_l]
+    for d in range(1, nl):
+        total = total + land_l[d - 1]
+    red[...] = total
+    whole = split == 1
+    copies = [
+        to_grp(red.at[0] if whole else red.at[lax.rem(me_g + d, ng)], land_g.at[d - 1], send_b, recv_b, d)
+        for d in range(1, ng)
+    ]
+    for c in copies:
+        c.start()
+    for c in copies:
+        c.wait()
+    if whole:
+        land_g[ng - 1] = red[0]
+        mine = land_g[lax.rem(me_g + ng - 1, ng)]
+        for g in range(1, ng):
+            mine = mine + land_g[lax.rem(me_g - g + 2 * ng - 1, ng)]
+        res[me_l, 0] = mine * factor
+    else:
+        mine = red[me_g]
+        for d in range(1, ng):
+            mine = mine + land_g[d - 1]
+        res[me_l, me_g] = mine * factor
+        piece = res.at[me_l, me_g]
+        copies = [to_grp(piece, piece, send_c, recv_c, d) for d in range(1, ng)]
+        for c in copies:
+            c.start()
+        for c in copies:
+            c.wait()
+    piece = res.at[me_l]
+    copies = [to_loop(piece, piece, send_d, recv_d, d) for d in range(1, nl)]
+    for c in copies:
+        c.start()
+    for c in copies:
+        c.wait()
+
+
+def reduce_kernel(nl, ng, split, factor, part, res, land_l, red, land_g, *sems):
+    greet(nl, ng)
+    reduce_all(nl, ng, split, factor, part, land_l, red, land_g, res, sems)
+
+
+def all_reduce(kterm, mterm, factor):
+    nl, ng = lax.axis_size("loop"), lax.axis_size("grp")
+    width = kterm.shape[1]
+    rows = 2 * kterm.shape[0] // nl
+    split = ng if rows % (8 * ng) == 0 else 1
+    rows = rows // split
+    part = jnp.concatenate([kterm, mterm], 0).reshape(nl, split, rows, width)
+    f32 = jnp.float32
+    vm = pl.BlockSpec(memory_space=pltpu.VMEM)
+    sem = pltpu.SemaphoreType.DMA
+    out = pl.pallas_call(
+        functools.partial(reduce_kernel, nl, ng, split, factor),
+        out_shape=jax.ShapeDtypeStruct(part.shape, f32),
+        in_specs=[vm],
+        out_specs=vm,
+        scratch_shapes=[
+            pltpu.VMEM((nl - 1, split, rows, width), f32),
+            pltpu.VMEM((split, rows, width), f32),
+            pltpu.VMEM((ng, rows, width), f32),
+        ] + [sem((n - 1,)) for n in (nl, nl, ng, ng, ng, ng, nl, nl)],
+        compiler_params=pltpu.CompilerParams(collective_id=0, has_side_effects=True),
+    )(part)
+    out = out.reshape(2, kterm.shape[0], width)
+    return out[0], out[1]
 
 
 def on_device(basis, stiffness, mass, col_index, live_counts):
@@ -57,10 +162,9 @@
     contract = (((0,), (0,)), ((), ()))
     kterm = lax.dot_general(basis, stiff_basis, contract, preferred_element_type=jnp.float32)
     mterm = lax.dot_general(basis, mass_basis, contract, preferred_element_type=jnp.float32)
-    kgram, mgram = lax.psum((kterm, mterm), ("loop", "grp"))
     total_dofs = basis.shape[0] * lax.axis_size("loop") * lax.axis_size("grp")
-    factor = jnp.float32(1.0) / jnp.sqrt(jnp.float32(total_dofs))
-    return (stiff_basis, mass_basis, kgram * factor, mgram * factor)
+    kgram, mgram = all_reduce(kterm, mterm, 1.0 / total_dofs**0.5)
+    return (stiff_basis, mass_basis, kgram, mgram)
 
 
 def solution(mesh):

time: 198 us -> 83.5 us (0.42)
  waiting for transfers between devices: 129 us -> 0.01 us
  Pallas kernels: 0 us -> 27 us
  between operations: 14.2 us -> 0.85 us
    psum x1 -> x0, waiting for transfers between devices: 129 us -> none  [on_device(): kgram, mgram = lax.psum((kterm, mterm), ('loop', 'grp'))]
    pallas_call x0 -> x1, Pallas kernels: none -> 27 us  [all_reduce(): pl.pallas_call(functools.partial(reduce_kernel, nl, ng, split, factor), o...]
  transfers between devices with their start and end apart: 4 -> 3, of which waited for: 1 -> 0; matrix products, arithmetic and copies ran while one was open for 19% -> 46% of each run, Pallas kernels for 0% -> 0%
where the time goes in v1:
time: 83.5 us; the launch traced here: 82.1 us
  local copies, waits for them, and re-layouts  29 us (35%)
  Pallas kernels  27 us (32%)
  matrix products  15.3 us (18%)
  other arithmetic  5.2 us (6%)
  starting transfers between devices  4.74 us (6%)
  between operations  0.85 us (1%)
    pallas_call x1, Pallas kernels, all_reduce(): pl.pallas_call(functools.partial(reduce_kernel, nl, ng, split, factor), o...  27 us
    gather x5, local copies, waits for them, and re-layouts, on_device(): picked = blocks[chosen]  13 us
    dot_general x5, matrix products, on_device(): jnp.einsum('rjab,rjbc->rac', mb[:, first:first + count], picked, preferre...  9.95 us
    reshape x1, local copies, waits for them, and re-layouts, on_device(): kb = stiffness.reshape(rows_dev, NB, BS, BS)  5.57 us
    dot_general x5, matrix products, on_device(): jnp.einsum('rjab,rjbc->rac', kb[:, first:first + count], picked, preferre...  4.75 us
    ppermute x3, starting transfers between devices, shifted(): return lax.ppermute(block, axis, route)  4.74 us
    reshape x1, local copies, waits for them, and re-layouts, on_device(): mb = mass.reshape(rows_dev, NB, BS, BS)  4.31 us
    unnamed x40, local copies, waits for them, and re-layouts  2.49 us
  transfers between devices with their start and end apart: 3, of which 0 were waited for; matrix products, arithmetic and copies ran while one was open for 46% of the time, Pallas kernels for 0%

profile of v1, /device:TPU:0, one launch (start us, length us, event | category | flops | bytes accessed | tf_op | source)
XLA Modules:
  0.0 82.1 jit_solution(8581331377793119784)
XLA Ops:
  1.1 2.0 %collective-permute-start = (bf16[768,256]{1,0:T(8,128)(2,1)}, bf16[768,256]{1,0:T(8,128)(2,1)}, u32[]{:S(2)}, u32[]{:S(2)}) collective-permute-start(bf16[768,256]{1,0:T(8,128)(2,1)} %param.5), channel_id=1, source_target_pairs={{8,0},{16,8},{24,16},{0,24},{9,1},{17,9},{25,17},{1,25},{10,2},{18... | collective-permute-start | bytes 1179656 | tf_op jit(solution)/shard_map/ppermute | solution.py:20
  3.1 2.2 %collective-permute-start.2 = (bf16[768,256]{1,0:T(8,128)(2,1)}, bf16[768,256]{1,0:T(8,128)(2,1)}, u32[]{:S(2)}, u32[]{:S(2)}) collective-permute-start(bf16[768,256]{1,0:T(8,128)(2,1)} %param.5), channel_id=1, source_target_pairs={{16,0},{24,8},{0,16},{8,24},{17,1},{25,9},{1,17},{9,25},{18,2},{26... | collective-permute-start | bytes 1179656 | tf_op jit(solution)/shard_map/ppermute | solution.py:20
  5.4 0.8 %compare_select_fusion.3 = (s32[12,3]{1,0:T(8,128)S(1)}, s32[12,3]{1,0:T(8,128)S(1)}) fusion(s32[12,16]{1,0:T(8,128)} %param.8), kind=kLoop, calls=%fused_computation.48 | loop fusion | flops 216 | bytes 576 | tf_op jit(solution)/shard_map/select_n | solution.py:144
  6.9 0.7 iota_compare_fusion
  9.0 0.8 %compare_select_fusion.1 = (s32[12,2]{1,0:T(8,128)S(1)}, s32[12,2]{1,0:T(8,128)S(1)}) fusion(s32[12,16]{1,0:T(8,128)} %param.8), kind=kLoop, calls=%fused_computation.46 | loop fusion | flops 144 | bytes 384 | tf_op jit(solution)/shard_map/select_n | solution.py:144
  9.8 4.3 %reshape.50 = bf16[12,16,64,64]{3,2,1,0:T(8,128)(2,1)S(1)} reshape(bf16[12,16,4096]{2,1,0:T(8,128)(2,1)} %param.7) | data formatting | bytes 3145728 | tf_op jit(solution)/shard_map/reshape | solution.py:128
  15.8 5.6 %reshape.46 = bf16[12,16,64,64]{3,2,1,0:T(8,128)(2,1)} reshape(bf16[12,16,4096]{2,1,0:T(8,128)(2,1)} %param.6) | data formatting | bytes 3145728 | tf_op jit(solution)/shard_map/reshape | solution.py:127
  21.4 2.4 %gather_fusion = bf16[72,64,256]{2,1,0:T(8,128)(2,1)} fusion(bf16[12,64,256]{2,1,0:T(8,128)(2,1)S(1)} %bitcast.87, s32[1024]{0:T(1024)S(1)} %pad_clamp_fusion.4), kind=kCustom, calls=%fused_computation | custom fusion | bytes 4718880 | tf_op jit(solution)/shard_map/gather | solution.py:144
  23.7 3.3 %fusion.2 = f32[12,256,64]{1,2,0:T(8,128)} fusion(bf16[12,16,64,64]{3,2,1,0:T(8,128)(2,1)S(1)} %reshape.50, bf16[12,6,64,256]{3,2,1,0:T(8,128)(2,1)} %bitcast.94, pred[12,6]{1,0:T(8,128)(4,1)S(1)} %bitcast.105), kind=kOutput, calls=%fused_computation.8 | convolution fusion | flops 152174592 | bytes 4718664 | tf_op jit(solution)/shard_map/rjab,rjbc->rac/dot_general | solution.py:152
  27.1 1.5 %fusion.3 = f32[12,256,64]{1,2,0:T(8,128)} fusion(bf16[12,16,64,64]{3,2,1,0:T(8,128)(2,1)S(1)} %copy-done.1, bf16[12,6,64,256]{3,2,1,0:T(8,128)(2,1)S(1)} %bitcast.95, pred[12,6]{1,0:T(8,128)(4,1)S(1)} %bitcast.106), kind=kOutput, calls=%fused_computation.9 | convolution fusion | flops 152174592 | bytes 4718664 | tf_op jit(solution)/shard_map/rjab,rjbc->rac/dot_general | solution.py:146
  28.6 2.5 %gather_fusion.4 = bf16[24,64,256]{2,1,0:T(8,128)(2,1)} fusion(bf16[12,64,256]{2,1,0:T(8,128)(2,1)} %bitcast.12, s32[1024]{0:T(1024)S(1)} %copy-done.15), kind=kCustom, calls=%fused_computation.4 | custom fusion | bytes 1572960 | tf_op jit(solution)/shard_map/gather | solution.py:144
  31.1 2.6 %gather_fusion.3 = bf16[24,64,256]{2,1,0:T(8,128)(2,1)} fusion(bf16[12,64,256]{2,1,0:T(8,128)(2,1)} %bitcast.12, s32[1024]{0:T(1024)} %pad_clamp_fusion.1), kind=kCustom, calls=%fused_computation.3 | custom fusion | bytes 1572960 | tf_op jit(solution)/shard_map/gather | solution.py:144
  33.8 2.8 %gather_fusion.2 = bf16[36,64,256]{2,1,0:T(8,128)(2,1)} fusion(bf16[12,64,256]{2,1,0:T(8,128)(2,1)} %bitcast.8, s32[1024]{0:T(1024)S(1)} %pad_clamp_fusion.2), kind=kCustom, calls=%fused_computation.2 | custom fusion | bytes 2359440 | tf_op jit(solution)/shard_map/gather | solution.py:144
  36.5 2.7 %convolution_bitcast_fusion.4 = f32[12,256,64]{1,2,0:T(8,128)} fusion(bf16[12,16,64,64]{3,2,1,0:T(8,128)(2,1)S(1)} %reshape.50, bf16[12,3,64,256]{3,2,1,0:T(8,128)(2,1)} %bitcast.101, pred[12,3]{1,0:T(8,128)(4,1)S(1)} %copy-done.19), kind=kOutput, calls=%fused_computation.14 | convolution fusion | flops 76087296 | bytes 3538980 | tf_op jit(solution)/shard_map/rjab,rjbc->rac/dot_general | solution.py:152
  39.3 1.3 %convolution_bitcast_fusion = f32[12,256,64]{1,2,0:T(8,128)} fusion(bf16[12,16,64,64]{3,2,1,0:T(8,128)(2,1)S(1)} %reshape.50, bf16[12,2,64,256]{3,2,1,0:T(8,128)(2,1)S(1)} %bitcast.92, pred[12,2]{1,0:T(8,128)(4,1)S(1)} %copy-done.18), kind=kOutput, calls=%fused_computation.10 | convolution fusion | flops 50724864 | bytes 3145752 | tf_op jit(solution)/shard_map/rjab,rjbc->rac/dot_general | solution.py:152
  40.6 1.2 %convolution_bitcast_fusion.2 = f32[12,256,64]{1,2,0:T(8,128)} fusion(bf16[12,16,64,64]{3,2,1,0:T(8,128)(2,1)S(1)} %copy-done.2, bf16[12,2,64,256]{3,2,1,0:T(8,128)(2,1)S(1)} %bitcast.93, pred[12,2]{1,0:T(8,128)(4,1)S(1)} %copy-done.18), kind=kOutput, calls=%fused_computation.12 | convolution fusion | flops 50724864 | bytes 3145752 | tf_op jit(solution)/shard_map/rjab,rjbc->rac/dot_general | solution.py:146
  41.8 1.3 %convolution_bitcast_fusion.6 = f32[12,256,64]{1,2,0:T(8,128)} fusion(bf16[12,16,64,64]{3,2,1,0:T(8,128)(2,1)S(1)} %copy-done.2, bf16[12,3,64,256]{3,2,1,0:T(8,128)(2,1)S(1)} %bitcast.102, pred[12,3]{1,0:T(8,128)(4,1)S(1)} %copy-done.19), kind=kOutput, calls=%fused_computation.16 | convolution fusion | flops 76087296 | bytes 3538980 | tf_op jit(solution)/shard_map/rjab,rjbc->rac/dot_general | solution.py:146
  43.1 2.7 %gather_fusion.1 = bf16[36,64,256]{2,1,0:T(8,128)(2,1)} fusion(bf16[12,64,256]{2,1,0:T(8,128)(2,1)} %bitcast.4, s32[1024]{0:T(1024)S(1)} %pad_clamp_fusion.3), kind=kCustom, calls=%fused_computation.1 | custom fusion | bytes 2359440 | tf_op jit(solution)/shard_map/gather | solution.py:144
  45.8 2.3 %fusion.11 = f32[12,256,64]{1,2,0:T(8,128)S(1)} fusion(f32[12,256,64]{1,2,0:T(8,128)} %convolution_bitcast_fusion.4, f32[12,256,64]{1,2,0:T(8,128)} %fusion.2, bf16[12,16,64,64]{3,2,1,0:T(8,128)(2,1)S(1)} %reshape.50, bf16[12,3,64,256]{3,2,1,0:T(8,128)(2,1)} %bitcast.88, pred[12,3]{1,0:T(8,128)(4,1)S(1)} %copy-done.17), kind=kOutput, calls=%fused_computation.25 | convolution fusion | flops 76480512 | bytes 5111844 | tf_op jit(solution)/shard_map/rjab,rjbc->rac/dot_general | solution.py:152
  48.9 1.4 %copy-done.3 = bf16[12,16,64,64]{3,2,1,0:T(8,128)(2,1)S(1)} copy-done((bf16[12,16,64,64]{3,2,1,0:T(8,128)(2,1)S(1)}, bf16[12,16,64,64]{3,2,1,0:T(8,128)(2,1)}, u32[]{:S(2)}) %copy-start.3) | copy-done | bytes 1572888
  51.0 0.7 copy-done.7
  52.4 0.8 %pad_maximum_fusion = f32[512,256]{1,0:T(8,128)} fusion(f32[256,256]{1,0:T(8,128)S(1)} %convolution_bitcast_fusion.8, f32[256,256]{1,0:T(8,128)S(1)} %convolution_bitcast_fusion.9), kind=kLoop, calls=%fused_computation.40 | loop fusion | flops 131072 | bytes 1048576 | tf_op jit(solution)/shard_map/concatenate | solution.py:104
  53.2 27.0 %shard_map.84 = f32[4,8,16,256]{3,2,1,0:T(8,128)} custom-call(f32[4,8,16,256]{3,2,1,0:T(8,128)} %bitcast.96), custom_call_target="tpu_custom_call" | custom-call | tf_op jit(solution)/shard_map/pallas_call | solution.py:108
  80.2 1.9 %fusion.34 = (f32[2,8,16,256]{3,2,1,0:T(8,128)}, f32[2,8,16,256]{3,2,1,0:T(8,128)}) fusion(f32[4,8,16,256]{3,2,1,0:T(8,128)} %shard_map.84), kind=kLoop, calls=%fused_computation.66 | loop fusion | bytes 1048576 | tf_op jit(solution)/shard_map/slice | solution.py:121
  (60 shorter events, 6.3 us)
Async XLA Ops:
  0.6 33.1 %collective-permute-start.1 = (bf16[768,256]{1,0:T(8,128)(2,1)}, bf16[768,256]{1,0:T(8,128)(2,1)}, u32[]{:S(2)}, u32[]{:S(2)}) collective-permute-start(bf16[768,256]{1,0:T(8,128)(2,1)} %param.5), channel_id=1, source_target_pairs={{24,0},{0,8},{8,16},{16,24},{25,1},{1,9},{9,17},{17,25},{26,2},{2,... | collective-permute-start | bytes 1179656 | tf_op jit(solution)/shard_map/ppermute | solution.py:20
  1.1 41.9 %collective-permute-start = (bf16[768,256]{1,0:T(8,128)(2,1)}, bf16[768,256]{1,0:T(8,128)(2,1)}, u32[]{:S(2)}, u32[]{:S(2)}) collective-permute-start(bf16[768,256]{1,0:T(8,128)(2,1)} %param.5), channel_id=1, source_target_pairs={{8,0},{16,8},{24,16},{0,24},{9,1},{17,9},{25,17},{1,25},{10,2},{18... | collective-permute-start | bytes 1179656 | tf_op jit(solution)/shard_map/ppermute | solution.py:20
  3.1 25.4 %collective-permute-start.2 = (bf16[768,256]{1,0:T(8,128)(2,1)}, bf16[768,256]{1,0:T(8,128)(2,1)}, u32[]{:S(2)}, u32[]{:S(2)}) collective-permute-start(bf16[768,256]{1,0:T(8,128)(2,1)} %param.5), channel_id=1, source_target_pairs={{16,0},{24,8},{0,16},{8,24},{17,1},{25,9},{1,17},{9,25},{18,2},{26... | collective-permute-start | bytes 1179656 | tf_op jit(solution)/shard_map/ppermute | solution.py:20
  15.8 5.6 %copy-start = (bf16[768,256]{1,0:T(8,128)(2,1)S(1)}, bf16[768,256]{1,0:T(8,128)(2,1)}, u32[]{:S(2)}) copy-start(bf16[768,256]{1,0:T(8,128)(2,1)} %param.5) | copy-start | bytes 1179652
  23.7 3.3 %copy-start.1 = (bf16[12,16,64,64]{3,2,1,0:T(8,128)(2,1)S(1)}, bf16[12,16,64,64]{3,2,1,0:T(8,128)(2,1)}, u32[]{:S(2)}) copy-start(bf16[12,16,64,64]{3,2,1,0:T(8,128)(2,1)} %reshape.46) | copy-start | bytes 4718596
  23.7 3.3 %copy-start.9 = (bf16[72,64,256]{2,1,0:T(8,128)(2,1)S(1)}, bf16[72,64,256]{2,1,0:T(8,128)(2,1)}, u32[]{:S(2)}) copy-start(bf16[72,64,256]{2,1,0:T(8,128)(2,1)} %gather_fusion) | copy-start | bytes 7077892
  27.1 1.5 %copy-start.15 = (s32[1024]{0:T(1024)S(1)}, s32[1024]{0:T(1024)}, u32[]{:S(2)}) copy-start(s32[1024]{0:T(1024)} %pad_clamp_fusion) | copy-start | bytes 12292
  31.1 5.4 %copy-start.19 = (pred[12,3]{1,0:T(8,128)(4,1)S(1)}, pred[12,3]{1,0:T(8,128)(4,1)}, u32[]{:S(2)}) copy-start(pred[12,3]{1,0:T(8,128)(4,1)} %get-tuple-element.13) | copy-start | bytes 112
  33.8 5.5 %copy-start.18 = (pred[12,2]{1,0:T(8,128)(4,1)S(1)}, pred[12,2]{1,0:T(8,128)(4,1)}, u32[]{:S(2)}) copy-start(pred[12,2]{1,0:T(8,128)(4,1)} %get-tuple-element.11) | copy-start | bytes 76
  36.5 2.7 %copy-start.6 = (bf16[24,64,256]{2,1,0:T(8,128)(2,1)S(1)}, bf16[24,64,256]{2,1,0:T(8,128)(2,1)}, u32[]{:S(2)}) copy-start(bf16[24,64,256]{2,1,0:T(8,128)(2,1)} %gather_fusion.4) | copy-start | bytes 2359300
  36.5 4.0 %copy-start.2 = (bf16[12,16,64,64]{3,2,1,0:T(8,128)(2,1)S(1)}, bf16[12,16,64,64]{3,2,1,0:T(8,128)(2,1)}, u32[]{:S(2)}) copy-start(bf16[12,16,64,64]{3,2,1,0:T(8,128)(2,1)} %reshape.46) | copy-start | bytes 4718596
  39.3 2.5 %copy-start.12 = (bf16[36,64,256]{2,1,0:T(8,128)(2,1)S(1)}, bf16[36,64,256]{2,1,0:T(8,128)(2,1)}, u32[]{:S(2)}) copy-start(bf16[36,64,256]{2,1,0:T(8,128)(2,1)} %gather_fusion.2) | copy-start | bytes 3538948
  41.8 4.0 %copy-start.17 = (pred[12,3]{1,0:T(8,128)(4,1)S(1)}, pred[12,3]{1,0:T(8,128)(4,1)}, u32[]{:S(2)}) copy-start(pred[12,3]{1,0:T(8,128)(4,1)} %get-tuple-element.12) | copy-start | bytes 112
  45.8 2.3 %copy-start.5 = (bf16[24,64,256]{2,1,0:T(8,128)(2,1)S(1)}, bf16[24,64,256]{2,1,0:T(8,128)(2,1)}, u32[]{:S(2)}) copy-start(bf16[24,64,256]{2,1,0:T(8,128)(2,1)} %gather_fusion.3) | copy-start | bytes 2359300
  45.8 2.3 %copy-start.8 = (f32[12,256,64]{1,2,0:T(8,128)S(1)}, f32[12,256,64]{1,2,0:T(8,128)}, u32[]{:S(2)}) copy-start(f32[12,256,64]{1,2,0:T(8,128)} %convolution_bitcast_fusion) | copy-start | bytes 2359300
  45.8 2.4 %copy-start.16 = (pred[12,2]{1,0:T(8,128)(4,1)S(1)}, pred[12,2]{1,0:T(8,128)(4,1)}, u32[]{:S(2)}) copy-start(pred[12,2]{1,0:T(8,128)(4,1)} %get-tuple-element.10) | copy-start | bytes 76
  45.8 3.0 %copy-start.13 = (f32[12,256,64]{1,2,0:T(8,128)S(1)}, f32[12,256,64]{1,2,0:T(8,128)}, u32[]{:S(2)}) copy-start(f32[12,256,64]{1,2,0:T(8,128)} %fusion.3) | copy-start | bytes 2359300
  45.8 3.0 %copy-start.14 = (f32[12,256,64]{1,2,0:T(8,128)S(1)}, f32[12,256,64]{1,2,0:T(8,128)}, u32[]{:S(2)}) copy-start(f32[12,256,64]{1,2,0:T(8,128)} %convolution_bitcast_fusion.6) | copy-start | bytes 2359300
  48.1 2.1 %copy-start.3 = (bf16[12,16,64,64]{3,2,1,0:T(8,128)(2,1)S(1)}, bf16[12,16,64,64]{3,2,1,0:T(8,128)(2,1)}, u32[]{:S(2)}) copy-start(bf16[12,16,64,64]{3,2,1,0:T(8,128)(2,1)} %reshape.46) | copy-start | bytes 4718596
  48.1 2.4 %copy-start.4 = (bf16[36,64,256]{2,1,0:T(8,128)(2,1)S(1)}, bf16[36,64,256]{2,1,0:T(8,128)(2,1)}, u32[]{:S(2)}) copy-start(bf16[36,64,256]{2,1,0:T(8,128)(2,1)} %gather_fusion.1) | copy-start | bytes 3538948
  48.5 2.5 %copy-start.10 = (bf16[12,256,64]{1,2,0:T(8,128)(2,1)}, bf16[12,256,64]{1,2,0:T(8,128)(2,1)S(1)}, u32[]{:S(2)}) copy-start(bf16[12,256,64]{1,2,0:T(8,128)(2,1)S(1)} %fusion.12) | copy-start | bytes 1179652
  50.6 1.1 %copy-start.7 = (f32[12,256,64]{1,2,0:T(8,128)S(1)}, f32[12,256,64]{1,2,0:T(8,128)}, u32[]{:S(2)}) copy-start(f32[12,256,64]{1,2,0:T(8,128)} %convolution_bitcast_fusion.2) | copy-start | bytes 2359300
  52.0 30.0 %copy-start.11 = (bf16[12,256,64]{1,2,0:T(8,128)(2,1)}, bf16[12,256,64]{1,2,0:T(8,128)(2,1)S(1)}, u32[]{:S(2)}) copy-start(bf16[12,256,64]{1,2,0:T(8,128)(2,1)S(1)} %fusion.13) | copy-start | bytes 1179652

commit v2 on v0

v2 whole, which is shorter than its diff:
```python
import functools

import jax
import jax.numpy as jnp
from jax import lax
from jax.experimental import pallas as pl
from jax.experimental.pallas import tpu as pltpu
from jax.sharding import PartitionSpec as P

BS = 64
NB = 16
LOCAL = 6
LANES = 128
GROUPS = 4
MESH = pl.DeviceIdType.MESH
BF16 = jnp.bfloat16
F32 = jnp.float32

SIB, AHEAD, FWD, BEHIND = range(4)


def fused_kernel(
    nl, ng, split, factor,
    col, live, basis, k_hbm, m_hbm,
    sbk, sbm, kgram, mgram,
    k_raw, m_raw, k_scr, m_scr, lhs, own, panels, basis_t, acc, tmp,
    part, land_c, half, land_q, red, land_g, res,
    own_sem, k_sem, m_sem, s_sib, r_sib, s_ahead, r_ahead, s_behind, r_behind, s_fwd, r_fwd,
    s_a1, r_a1, s_a2, r_a2, s_b, r_b, s_c, r_c, s_d1, r_d1, s_d2, r_d2,
):
    me_l, me_g = lax.axis_index("loop"), lax.axis_index("grp")
    nq = nl // 2
    me_q, me_c = me_l // 2, lax.rem(me_l, 2)
    n_rows = k_raw.shape[0]
    width = basis.shape[2]
    per = n_rows // GROUPS
    sibling = (2 * me_q + 1 - me_c, me_g)

    def chip(d):
        return (2 * lax.rem(me_q + d, nq) + me_c, me_g)

    def grp(d):
        return (me_l, lax.rem(me_g + d, ng))

    def send(src, dst, s, r, dev):
        return pltpu.make_async_remote_copy(
            src_ref=src, dst_ref=dst, send_sem=s, recv_sem=r, device_id=dev, device_id_type=MESH)

    own_load = pltpu.make_async_copy(basis, own.at[pl.ds(0, n_rows)], own_sem)
    own_load.start()
    loads = []
    for t in range(GROUPS):
        span = pl.ds(t * per, per)
        pair = (
            pltpu.make_async_copy(k_hbm.at[span], k_raw.at[span], k_sem.at[t]),
            pltpu.make_async_copy(m_hbm.at[span], m_raw.at[span], m_sem.at[t]),
        )
        for c in pair:
            c.start()
        loads.append(pair)

    barrier = pltpu.get_barrier_semaphore()
    pl.semaphore_signal(barrier, inc=1, device_id=sibling, device_id_type=MESH)
    for d in range(1, nq):
        pl.semaphore_signal(barrier, inc=1, device_id=chip(d), device_id_type=MESH)
    for d in range(1, ng):
        pl.semaphore_signal(barrier, inc=1, device_id=grp(d), device_id_type=MESH)
    pl.semaphore_wait(barrier, 1 + (nq - 1) + (ng - 1))

    two_ways = nq > 2
    ahead, behind, forward = [], [], []
    far = AHEAD if not two_ways else jnp.where(me_c == 0, AHEAD, BEHIND)
    for t in range(GROUPS):
        span = pl.ds(t * per, per)
        c = send(basis.at[span], panels.at[AHEAD, span], s_ahead.at[t], r_ahead.at[t], chip(nq - 1))
        c.start()
        ahead.append(c)
        if two_ways:
            c = send(basis.at[span], panels.at[BEHIND, span], s_behind.at[t], r_behind.at[t], chip(1))
            c.start()
            behind.append(c)
        forward.append(send(panels.at[far, span], panels.at[FWD, span], s_fwd.at[t], r_fwd.at[t], sibling))
    sib = send(basis, panels.at[SIB, pl.ds(0, n_rows)], s_sib, r_sib, sibling)
    sib.start()

    own[n_rows] = jnp.zeros((BS, width), BF16)
    for s in range(panels.shape[0]):
        panels[s, n_rows] = jnp.zeros((BS, width), BF16)

    low = lax.broadcasted_iota(jnp.int32, (BS // 2, LANES), 1) < BS

    def relayout(raw, scr, r, base):
        for p in range(BS // 2):
            scr[p * NB : (p + 1) * NB, :] = raw[r, :, p * LANES : (p + 1) * LANES].astype(F32)
        for j in range(NB // 2):
            even = scr[pl.ds(2 * j, BS // 2, stride=NB), :]
            odd = scr[pl.ds(2 * j + 1, BS // 2, stride=NB), :]
            first = jnp.where(low, even, pltpu.roll(odd, BS, 1))
            second = jnp.where(low, pltpu.roll(even, BS, 1), odd)
            lanes = slice(j * LANES, (j + 1) * LANES)
            lhs[r, base : base + BS // 2, lanes] = first.astype(BF16)
            lhs[r, base + BS // 2 : base + BS, lanes] = second.astype(BF16)

    for t in range(GROUPS):
        for c in loads[t]:
            c.wait()

        def rows(r, carry):
            relayout(k_raw, k_scr, r, 0)
            relayout(m_raw, m_scr, r, BS)
            return carry

        lax.fori_loop(t * per, (t + 1) * per, rows, 0)
        ahead[t].wait_recv()
        if two_ways:
            behind[t].wait_recv()
        forward[t].start()

    def block(r, s):
        return jnp.where(s < live[r], col[r, s], n_rows)

    own_load.wait()

    def local_rows(r, carry):
        rhs = jnp.concatenate([own[block(r, s)] for s in range(LOCAL)], 0)
        acc[r] = jnp.dot(lhs[r, :, : LOCAL * BS], rhs, preferred_element_type=F32)
        return carry

    lax.fori_loop(0, n_rows, local_rows, 0)
    basis_t[...] = own[:n_rows].reshape(n_rows * BS, width).T

    sib.wait()
    for t in range(GROUPS):
        ahead[t].wait_send()
        if two_ways:
            behind[t].wait_send()
        forward[t].wait()

    plus = jnp.where(me_c == 0, SIB, FWD)
    minus = jnp.where(me_c == 0, FWD, SIB)
    back = BEHIND if two_ways else AHEAD
    owners = [plus] * 3 + [minus] * 3 + [AHEAD] * 2 + [back] * 2

    def remote_rows(r, carry):
        rhs = jnp.concatenate([panels[o, block(r, LOCAL + s)] for s, o in enumerate(owners)], 0)
        out = acc[r] + jnp.dot(lhs[r, :, LOCAL * BS :], rhs, preferred_element_type=F32)
        h = BS // 2
        for m, dst in enumerate((sbk, sbm)):
            for w in range(width // LANES):
                i = m * (width // LANES) + w
                lanes = slice(w * LANES, (w + 1) * LANES)
                tmp[i, pl.ds(0, h, stride=2), :] = out[m * BS : m * BS + h, lanes]
                tmp[i, pl.ds(1, h, stride=2), :] = out[m * BS + h : (m + 1) * BS, lanes]
                dst[r, :, lanes] = tmp[i].astype(BF16)
        return carry

    lax.fori_loop(0, n_rows, remote_rows, 0)

    step = part.shape[3]
    pieces = width // step
    for m, src in enumerate((sbk, sbm)):
        gram = jnp.dot(basis_t[...], src[...].reshape(n_rows * BS, width), preferred_element_type=F32)
        for i in range(pieces):
            n = m * pieces + i
            part[n // (2 * split), n // split % 2, n % split] = gram[i * step : (i + 1) * step]

    c = send(part.at[:, 1 - me_c], land_c, s_a1, r_a1, sibling)
    c.start()
    c.wait()
    half[...] = part[:, me_c] + land_c[...]
    copies = [
        send(half.at[lax.rem(me_q + d, nq)], land_q.at[d - 1], s_a2.at[d - 1], r_a2.at[d - 1], chip(d))
        for d in range(1, nq)
    ]
    for c in copies:
        c.start()
    for c in copies:
        c.wait()
    total = half[me_q]
    for d in range(1, nq):
        total = total + land_q[d - 1]
    red[...] = total
    whole = split == 1
    copies = [
        send(red.at[0] if whole else red.at[lax.rem(me_g + d, ng)], land_g.at[d - 1], s_b.at[d - 1], r_b.at[d - 1], grp(d))
        for d in range(1, ng)
    ]
    for c in copies:
        c.start()
    for c in copies:
        c.wait()
    if whole:
        land_g[ng - 1] = red[0]
        mine = land_g[lax.rem(me_g + ng - 1, ng)]
        for g in range(1, ng):
            mine = mine + land_g[lax.rem(me_g - g + 2 * ng - 1, ng)]
        res[me_q, me_c, 0] = mine * factor
    else:
        mine = red[me_g]
        for d in range(1, ng):
            mine = mine + land_g[d - 1]
        res[me_q, me_c, me_g] = mine * factor
        piece = res.at[me_q, me_c, me_g]
        copies = [send(piece, piece, s_c.at[d - 1], r_c.at[d - 1], grp(d)) for d in range(1, ng)]
        for c in copies:
            c.start()
        for c in copies:
            c.wait()
    piece = res.at[me_q, me_c]
    copies = [send(piece, piece, s_d1.at[d - 1], r_d1.at[d - 1], chip(d)) for d in range(1, nq)]
    for c in copies:
        c.start()
    for c in copies:
        c.wait()
    piece = res.at[:, me_c]
    c = send(piece, piece, s_d2, r_d2, sibling)
    c.start()
    c.wait()
    for m, dst in enumerate((kgram, mgram)):
        for i in range(pieces):
            n = m * pieces + i
            dst[i * step : (i + 1) * step, :] = res[n // (2 * split), n // split % 2, n % split]


def on_device(basis, stiffness, mass, col_index, live_counts):
    nl, ng = lax.axis_size("loop"), lax.axis_size("grp")
    nq = nl // 2
    n_rows = stiffness.shape[0]
    width = basis.shape[1]
    step = 2 * width // nl
    split = ng if step % (8 * ng) == 0 else 1
    step = step // split
    factor = 1.0 / (basis.shape[0] * nl * ng) ** 0.5
    vmem, smem, hbm = (pl.BlockSpec(memory_space=s) for s in (pltpu.VMEM, pltpu.SMEM, pltpu.HBM))
    sem = pltpu.SemaphoreType.DMA
    sb = jax.ShapeDtypeStruct((n_rows, BS, width), BF16)
    gram = jax.ShapeDtypeStruct((width, width), F32)
    stiff, massb, kgram, mgram = pl.pallas_call(
        functools.partial(fused_kernel, nl, ng, split, factor),
        out_shape=(sb, sb, gram, gram),
        in_specs=[smem, smem, hbm, hbm, hbm],
        out_specs=(vmem,) * 4,
        scratch_shapes=[
            pltpu.VMEM(stiffness.shape, BF16),
            pltpu.VMEM(mass.shape, BF16),
            pltpu.VMEM((NB * BS // 2, LANES), F32),
            pltpu.VMEM((NB * BS // 2, LANES), F32),
            pltpu.VMEM((n_rows, 2 * BS, NB * BS), BF16),
            pltpu.VMEM((n_rows + 1, BS, width), BF16),
            pltpu.VMEM((4 if nq > 2 else 3, n_rows + 1, BS, width), BF16),
            pltpu.VMEM((width, n_rows * BS), BF16),
            pltpu.VMEM((n_rows, 2 * BS, width), F32),
            pltpu.VMEM((2 * width // LANES, BS, LANES), F32),
            pltpu.VMEM((nq, 2, split, step, width), F32),
            pltpu.VMEM((nq, split, step, width), F32),
            pltpu.VMEM((nq, split, step, width), F32),
            pltpu.VMEM((nq - 1, split, step, width), F32),
            pltpu.VMEM((split, step, width), F32),
            pltpu.VMEM((ng, step, width), F32),
            pltpu.VMEM((nq, 2, split, step, width), F32),
            sem(()), sem((GROUPS,)), sem((GROUPS,)), sem(()), sem(()),
            sem((GROUPS,)), sem((GROUPS,)), sem((GROUPS,)), sem((GROUPS,)), sem((GROUPS,)), sem((GROUPS,)),
            sem(()), sem(()), sem((nq - 1,)), sem((nq - 1,)),
            sem((ng - 1,)), sem((ng - 1,)), sem((ng - 1,)), sem((ng - 1,)),
            sem((nq - 1,)), sem((nq - 1,)), sem(()), sem(()),
        ],
        compiler_params=pltpu.CompilerParams(
            collective_id=0, has_side_effects=True, vmem_limit_bytes=40 * 1024 * 1024
        ),
    )(col_index, live_counts, basis.reshape(n_rows, BS, width), stiffness, mass)
    return (stiff.reshape(n_rows * BS, width), massb.reshape(n_rows * BS, width), kgram, mgram)


def solution(mesh):
    in_specs = (
        P(("loop", "grp"), None),
        P(("loop", "grp"), None, None),
        P(("loop", "grp"), None, None),
        P(("loop", "grp"), None),
        P(("loop", "grp")),
    )
    out_specs = (P(("loop", "grp"), None), P(("loop", "grp"), None), P(), P())
    return jax.shard_map(
        on_device, mesh=mesh, in_specs=in_specs, out_specs=out_specs, check_vma=False
    )
```

time: 198 us -> 54.5 us (0.28)
  waiting for transfers between devices: 129 us -> 0 us
  Pallas kernels: 0 us -> 45.5 us
  local copies, waits for them, and re-layouts: 28.2 us -> 8.05 us
  matrix products: 16.7 us -> 0 us
  between operations: 14.2 us -> 0.65 us
  other arithmetic: 5.42 us -> 0 us
  starting transfers between devices: 4.77 us -> 0 us
    psum x1 -> x0, waiting for transfers between devices: 129 us -> none  [on_device(): kgram, mgram = lax.psum((kterm, mterm), ('loop', 'grp'))]
    pallas_call x0 -> x1, Pallas kernels: none -> 45.5 us  [on_device(): pl.pallas_call(functools.partial(fused_kernel, nl, ng, split, factor), ou...]
    dot_general x12 -> x0, matrix products: 16.7 us -> none  [the longest x5 9.93 us: on_device(): jnp.einsum('rjab,rjbc->rac', mb[:, first:first + count], picked, preferre...]
    gather x5 -> x0, local copies, waits for them, and re-layouts: 13 us -> none  [on_device(): picked = blocks[chosen]]
    reshape x2 -> x0, local copies, waits for them, and re-layouts: 9.85 us -> none  [the longest x1 5.54 us: on_device(): kb = stiffness.reshape(rows_dev, NB, BS, BS)]
    ppermute x3 -> x0, starting transfers between devices: 4.74 us -> none  [shifted(): return lax.ppermute(block, axis, route)]
    unnamed x42 -> x14, local copies, waits for them, and re-layouts: 3.58 us -> 8.05 us
    select_n x3 -> x0, other arithmetic: 2.39 us -> none  [on_device(): picked = blocks[chosen]]
  transfers between devices with their start and end apart: 4 -> 0, of which waited for: 1 -> 0; matrix products, arithmetic and copies ran while one was open for 19% -> 0% of each run, Pallas kernels for 0% -> 0%
where the time goes in v2:
time: 54.5 us; the launch traced here: 54.2 us
  Pallas kernels  45.5 us (83%)
  local copies, waits for them, and re-layouts  8.05 us (15%)
  between operations  0.65 us (1%)
    pallas_call x1, Pallas kernels, on_device(): pl.pallas_call(functools.partial(fused_kernel, nl, ng, split, factor), ou...  45.5 us
    unnamed x14, local copies, waits for them, and re-layouts  8.05 us

profile of v2, /device:TPU:0, one launch (start us, length us, event | category | flops | bytes accessed | tf_op | source)
XLA Modules:
  0.0 54.2 jit_solution(4318424921908890705)
XLA Ops:
  0.6 0.0 copy-start
  0.6 1.4 %copy-done = bf16[12,16,4096]{2,1,0:T(8,128)(2,1)S(1)} copy-done((bf16[12,16,4096]{2,1,0:T(8,128)(2,1)S(1)}, bf16[12,16,4096]{2,1,0:T(8,128)(2,1)}, u32[]{:S(2)}) %copy-start) | copy-done | bytes 1572888
  2.0 0.0 copy-start.1
  2.0 1.4 %copy-done.1 = bf16[12,16,4096]{2,1,0:T(8,128)(2,1)S(1)} copy-done((bf16[12,16,4096]{2,1,0:T(8,128)(2,1)S(1)}, bf16[12,16,4096]{2,1,0:T(8,128)(2,1)}, u32[]{:S(2)}) %copy-start.1) | copy-done | bytes 1572888
  3.4 0.0 copy-start.2
  3.5 1.0 %copy-done.2 = bf16[768,256]{1,0:T(8,128)(2,1)S(1)} copy-done((bf16[768,256]{1,0:T(8,128)(2,1)S(1)}, bf16[768,256]{1,0:T(8,128)(2,1)}, u32[]{:S(2)}) %copy-start.2) | copy-done | bytes 393240
  4.4 0.0 copy-start.3
  4.4 0.7 %copy-done.3 = s32[12,16]{1,0:T(8,128)S(1)} copy-done((s32[12,16]{1,0:T(8,128)S(1)}, s32[12,16]{1,0:T(8,128)}, u32[]{:S(2)}) %copy-start.3) | copy-done | bytes 792
  5.1 0.0 copy-start.4
  5.1 0.7 %copy-done.4 = s32[12]{0:T(128)S(1)} copy-done((s32[12]{0:T(128)S(1)}, s32[12]{0:T(128)}, u32[]{:S(2)}) %copy-start.4) | copy-done | bytes 72
  5.8 45.5 %shard_map.84 = (bf16[12,64,256]{2,1,0:T(8,128)(2,1)S(1)}, bf16[12,64,256]{2,1,0:T(8,128)(2,1)S(1)}, f32[256,256]{1,0:T(8,128)S(1)}, f32[256,256]{1,0:T(8,128)S(1)}) custom-call(s32[12,16]{1,0:T(8,128)S(1)} %copy-done.3, s32[12]{0:T(128)S(1)} %copy-done.4, bf16[12,64,256]{2,1,0:T(8,128)(2,1)S(1)} %bitcast.5, bf16[12,16,4096]{2,1,0:T(8,128)(2,1)S(1)} %copy-done, ...), custom_call_target="tpu_custom_call" | custom-call | tf_op jit(solution)/shard_map/pallas_call | solution.py:238
  51.3 0.7 %copy.13 = bf16[768,256]{1,0:T(8,128)(2,1)} copy(bf16[768,256]{1,0:T(8,128)(2,1)S(1)} %bitcast.4) | data formatting | bytes 786432
  52.1 0.7 %copy.14 = bf16[768,256]{1,0:T(8,128)(2,1)} copy(bf16[768,256]{1,0:T(8,128)(2,1)S(1)} %bitcast.3) | data formatting | bytes 786432
  52.8 0.7 %copy.15 = f32[256,256]{1,0:T(8,128)} copy(f32[256,256]{1,0:T(8,128)S(1)} %get-tuple-element.18) | data formatting | bytes 524288
  53.5 0.7 %copy.16 = f32[256,256]{1,0:T(8,128)} copy(f32[256,256]{1,0:T(8,128)S(1)} %get-tuple-element.19) | data formatting | bytes 524288
Async XLA Ops:
  0.6 1.4 %copy-start = (bf16[12,16,4096]{2,1,0:T(8,128)(2,1)S(1)}, bf16[12,16,4096]{2,1,0:T(8,128)(2,1)}, u32[]{:S(2)}) copy-start(bf16[12,16,4096]{2,1,0:T(8,128)(2,1)} %k_hbm.1) | copy-start | bytes 4718596
  2.0 1.4 %copy-start.1 = (bf16[12,16,4096]{2,1,0:T(8,128)(2,1)S(1)}, bf16[12,16,4096]{2,1,0:T(8,128)(2,1)}, u32[]{:S(2)}) copy-start(bf16[12,16,4096]{2,1,0:T(8,128)(2,1)} %m_hbm.1) | copy-start | bytes 4718596
  3.4 1.0 %copy-start.2 = (bf16[768,256]{1,0:T(8,128)(2,1)S(1)}, bf16[768,256]{1,0:T(8,128)(2,1)}, u32[]{:S(2)}) copy-start(bf16[768,256]{1,0:T(8,128)(2,1)} %param.5) | copy-start | bytes 1179652
  4.4 0.7 %copy-start.3 = (s32[12,16]{1,0:T(8,128)S(1)}, s32[12,16]{1,0:T(8,128)}, u32[]{:S(2)}) copy-start(s32[12,16]{1,0:T(8,128)} %col.1) | copy-start | bytes 2308
  5.1 0.7 %copy-start.4 = (s32[12]{0:T(128)S(1)}, s32[12]{0:T(128)}, u32[]{:S(2)}) copy-start(s32[12]{0:T(128)} %live.1) | copy-start | bytes 148

commit v3 on v2

v3 whole, which is shorter than its diff:
```python
import functools

import jax
import jax.numpy as jnp
from jax import lax
from jax.experimental import pallas as pl
from jax.experimental.pallas import tpu as pltpu
from jax.sharding import PartitionSpec as P

BS = 64
NB = 16
LOCAL = 6
LANES = 128
GROUPS = 4
HALVES = 2
CHUNKS = 2
MESH = pl.DeviceIdType.MESH
BF16 = jnp.bfloat16
F32 = jnp.float32

SIB, AHEAD, FWD, BEHIND = range(4)


def fused_kernel(
    nl, ng, split, factor,
    col, live, basis, k_hbm, m_hbm,
    sbk, sbm, kgram, mgram,
    k_raw, m_raw, k_scr, m_scr, lhs, own, panels0, panels1, basis_t, acc, tmp, stiff, massb,
    part, land_c, half, land_q, red, land_g, res,
    own_sem, k_sem, m_sem, out_sem, s_sib, r_sib, s_ahead, r_ahead, s_behind, r_behind, s_fwd, r_fwd,
    s_a1, r_a1, s_a2, r_a2, s_b, r_b, s_c, r_c, s_d1, r_d1, s_d2, r_d2,
):
    me_l, me_g = lax.axis_index("loop"), lax.axis_index("grp")
    nq = nl // 2
    me_q, me_c = me_l // 2, lax.rem(me_l, 2)
    n_rows = k_raw.shape[0]
    panels = (panels0, panels1)
    per = n_rows // GROUPS
    chunk = n_rows // CHUNKS
    sibling = (2 * me_q + 1 - me_c, me_g)
    whole = split == 1

    def chip(d):
        return (2 * lax.rem(me_q + d, nq) + me_c, me_g)

    def grp(d):
        return (me_l, lax.rem(me_g + d, ng))

    def send(src, dst, s, r, dev):
        return pltpu.make_async_remote_copy(
            src_ref=src, dst_ref=dst, send_sem=s, recv_sem=r, device_id=dev, device_id_type=MESH)

    def lanes(w):
        return pl.ds(w * LANES, LANES)

    own_loads = [
        pltpu.make_async_copy(basis.at[:, :, lanes(w)], own.at[w, pl.ds(0, n_rows)], own_sem.at[w])
        for w in range(HALVES)
    ]
    for c in own_loads:
        c.start()
    barrier = pltpu.get_barrier_semaphore()
    pl.semaphore_signal(barrier, inc=1, device_id=sibling, device_id_type=MESH)
    for d in range(1, nq):
        pl.semaphore_signal(barrier, inc=1, device_id=chip(d), device_id_type=MESH)
    for d in range(1, ng):
        pl.semaphore_signal(barrier, inc=1, device_id=grp(d), device_id_type=MESH)
    loads = []
    for t in range(GROUPS):
        span = pl.ds(t * per, per)
        pair = (
            pltpu.make_async_copy(k_hbm.at[span], k_raw.at[span], k_sem.at[t]),
            pltpu.make_async_copy(m_hbm.at[span], m_raw.at[span], m_sem.at[t]),
        )
        for c in pair:
            c.start()
        loads.append(pair)
    zero = jnp.zeros((BS, LANES), BF16)
    for w in range(HALVES):
        own[w, n_rows] = zero
        for s in range(panels[w].shape[0]):
            panels[w][s, n_rows] = zero
    for c in own_loads:
        c.wait()
    pl.semaphore_wait(barrier, 1 + (nq - 1) + (ng - 1))

    two_ways = nq > 2
    far = AHEAD if not two_ways else jnp.where(me_c == 0, AHEAD, BEHIND)
    arrive, forward, sib = [], [], []
    for w in range(HALVES):
        for t in range(CHUNKS):
            span = pl.ds(t * chunk, chunk)
            src = own.at[w, span]
            pair = [send(src, panels[w].at[AHEAD, span], s_ahead.at[w, t], r_ahead.at[w, t], chip(nq - 1))]
            if two_ways:
                pair.append(send(src, panels[w].at[BEHIND, span], s_behind.at[w, t], r_behind.at[w, t], chip(1)))
            for c in pair:
                c.start()
            arrive.append(pair)
            forward.append(
                send(panels[w].at[far, span], panels[w].at[FWD, span], s_fwd.at[w, t], r_fwd.at[w, t], sibling))
        sib.append(
            send(own.at[w, pl.ds(0, n_rows)], panels[w].at[SIB, pl.ds(0, n_rows)], s_sib.at[w], r_sib.at[w], sibling))
        sib[w].start()

    def pass_on(i):
        for c in arrive[i]:
            c.wait_recv()
        forward[i].start()

    low = lax.broadcasted_iota(jnp.int32, (BS // 2, LANES), 1) < BS

    def relayout(raw, scr, r, base):
        for p in range(BS // 2):
            scr[p * NB : (p + 1) * NB, :] = raw[r, :, p * LANES : (p + 1) * LANES].astype(F32)
        for j in range(NB // 2):
            even = scr[pl.ds(2 * j, BS // 2, stride=NB), :]
            odd = scr[pl.ds(2 * j + 1, BS // 2, stride=NB), :]
            first = jnp.where(low, even, pltpu.roll(odd, BS, 1))
            second = jnp.where(low, pltpu.roll(even, BS, 1), odd)
            at = slice(j * LANES, (j + 1) * LANES)
            lhs[r, base : base + BS // 2, at] = first.astype(BF16)
            lhs[r, base + BS // 2 : base + BS, at] = second.astype(BF16)

    for t in range(GROUPS):
        for c in loads[t]:
            c.wait()

        def rows(r, carry):
            relayout(k_raw, k_scr, r, 0)
            relayout(m_raw, m_scr, r, BS)
            return carry

        lax.fori_loop(t * per, (t + 1) * per, rows, 0)
        if t % 2 == 1 and t // 2 < CHUNKS:
            pass_on(t // 2)

    def block(r, s):
        return jnp.where(s < live[r], col[r, s], n_rows)

    def local_rows(r, carry):
        for w in range(HALVES):
            rhs = jnp.concatenate([own[w, block(r, s)] for s in range(LOCAL)], 0)
            acc[w, r] = jnp.dot(lhs[r, :, : LOCAL * BS], rhs, preferred_element_type=F32)
        return carry

    lax.fori_loop(0, n_rows, local_rows, 0)
    for w in range(HALVES):
        basis_t[w * LANES : (w + 1) * LANES, :] = own[w, :n_rows].reshape(n_rows * BS, LANES).T

    plus = jnp.where(me_c == 0, SIB, FWD)
    minus = jnp.where(me_c == 0, FWD, SIB)
    back = BEHIND if two_ways else AHEAD
    owners = [plus] * 3 + [minus] * 3 + [AHEAD] * 2 + [back] * 2
    step = part.shape[4]
    pieces = 2 * HALVES * LANES // step // 2
    outs = []

    def products(w):
        sib[w].wait()
        for t in range(CHUNKS):
            for c in arrive[w * CHUNKS + t]:
                c.wait_send()
            forward[w * CHUNKS + t].wait()

        def remote_rows(r, carry):
            rhs = jnp.concatenate([panels[w][o, block(r, LOCAL + s)] for s, o in enumerate(owners)], 0)
            out = acc[w, r] + jnp.dot(lhs[r, :, LOCAL * BS :], rhs, preferred_element_type=F32)
            h = BS // 2
            for m, dst in enumerate((stiff, massb)):
                tmp[m, pl.ds(0, h, stride=2), :] = out[m * BS : m * BS + h]
                tmp[m, pl.ds(1, h, stride=2), :] = out[m * BS + h : (m + 1) * BS]
                dst[w, r] = tmp[m].astype(BF16)
            return carry

        lax.fori_loop(0, n_rows, remote_rows, 0)
        for m, (src, dst) in enumerate(((stiff, sbk), (massb, sbm))):
            gram = jnp.dot(basis_t[...], src[w].reshape(n_rows * BS, LANES), preferred_element_type=F32)
            for i in range(pieces):
                n = m * pieces + i
                part[w, n // (2 * split), n // split % 2, n % split] = gram[i * step : (i + 1) * step]

    def store(w):
        for m, (src, dst) in enumerate(((stiff, sbk), (massb, sbm))):
            c = pltpu.make_async_copy(src.at[w], dst.at[:, :, lanes(w)], out_sem.at[w, m])
            c.start()
            outs.append(c)

    def stages(w):
        def to_sibling():
            return [send(part.at[w, :, 1 - me_c], land_c.at[w], s_a1.at[w], r_a1.at[w], sibling)]

        def to_chips():
            half[w] = part[w, :, me_c] + land_c[w]
            return [
                send(half.at[w, lax.rem(me_q + d, nq)], land_q.at[w, d - 1], s_a2.at[w, d - 1], r_a2.at[w, d - 1], chip(d))
                for d in range(1, nq)
            ]

        def to_group():
            total = half[w, me_q]
            for d in range(1, nq):
                total = total + land_q[w, d - 1]
            red[w] = total
            return [
                send(
                    red.at[w, 0] if whole else red.at[w, lax.rem(me_g + d, ng)],
                    land_g.at[w, d - 1], s_b.at[w, d - 1], r_b.at[w, d - 1], grp(d))
                for d in range(1, ng)
            ]

        def from_group():
            if whole:
                land_g[w, ng - 1] = red[w, 0]
                mine = land_g[w, lax.rem(me_g + ng - 1, ng)]
                for g in range(1, ng):
                    mine = mine + land_g[w, lax.rem(me_g - g + 2 * ng - 1, ng)]
                res[w, me_q, me_c, 0] = mine * factor
                return []
            mine = red[w, me_g]
            for d in range(1, ng):
                mine = mine + land_g[w, d - 1]
            res[w, me_q, me_c, me_g] = mine * factor
            piece = res.at[w, me_q, me_c, me_g]
            return [send(piece, piece, s_c.at[w, d - 1], r_c.at[w, d - 1], grp(d)) for d in range(1, ng)]

        def from_chips():
            piece = res.at[w, me_q, me_c]
            return [send(piece, piece, s_d1.at[w, d - 1], r_d1.at[w, d - 1], chip(d)) for d in range(1, nq)]

        def from_sibling():
            piece = res.at[w, :, me_c]
            return [send(piece, piece, s_d2.at[w], r_d2.at[w], sibling)]

        for stage in (to_sibling, to_chips, to_group, from_group, from_chips, from_sibling):
            copies = stage()
            for c in copies:
                c.start()
            yield
            for c in copies:
                c.wait()
        for m, dst in enumerate((kgram, mgram)):
            for i in range(pieces):
                n = m * pieces + i
                dst[i * step : (i + 1) * step, w * LANES : (w + 1) * LANES] = res[
                    w, n // (2 * split), n // split % 2, n % split]

    first, second = stages(0), stages(1)
    products(0)
    next(first)
    store(0)
    pass_on(CHUNKS)
    next(first)
    for t in range(1, CHUNKS):
        pass_on(CHUNKS + t)
    next(first)
    products(1)
    next(second)
    store(1)
    for _ in range(3):
        next(first)
        next(second)
    next(first, None)
    for _ in second:
        pass
    for c in outs:
        c.wait()


def copy_kernel(*refs):
    n = len(refs) // 2
    copies = [pltpu.make_async_copy(refs[i], refs[n + i], refs[-1].at[i]) for i in range(n)]
    for c in copies:
        c.start()
    for c in copies:
        c.wait()


def on_device(basis, stiffness, mass, col_index, live_counts):
    nl, ng = lax.axis_size("loop"), lax.axis_size("grp")
    nq = nl // 2
    n_rows = stiffness.shape[0]
    width = basis.shape[1]
    step = 2 * width // nl
    split = ng if step % (8 * ng) == 0 else 1
    step = step // split
    factor = 1.0 / (basis.shape[0] * nl * ng) ** 0.5
    vmem, smem, hbm = (pl.BlockSpec(memory_space=s) for s in (pltpu.VMEM, pltpu.SMEM, pltpu.HBM))
    sem = pltpu.SemaphoreType.DMA
    sb = jax.ShapeDtypeStruct((n_rows, BS, width), BF16)
    gram = jax.ShapeDtypeStruct((width, width), F32)
    panel = pltpu.VMEM((4 if nq > 2 else 3, n_rows + 1, BS, LANES), BF16)

    def f32(*shape):
        return pltpu.VMEM(shape, F32)

    def sems(n, *shape):
        return [sem(shape)] * n

    outs = pl.pallas_call(
        functools.partial(fused_kernel, nl, ng, split, factor),
        out_shape=(sb, sb, gram, gram),
        in_specs=[smem, smem, hbm, hbm, hbm],
        out_specs=(hbm, hbm, vmem, vmem),
        scratch_shapes=[
            pltpu.VMEM(stiffness.shape, BF16),
            pltpu.VMEM(mass.shape, BF16),
            f32(NB * BS // 2, LANES),
            f32(NB * BS // 2, LANES),
            pltpu.VMEM((n_rows, 2 * BS, NB * BS), BF16),
            pltpu.VMEM((HALVES, n_rows + 1, BS, LANES), BF16),
            panel,
            panel,
            pltpu.VMEM((width, n_rows * BS), BF16),
            f32(HALVES, n_rows, 2 * BS, LANES),
            f32(2, BS, LANES),
            pltpu.VMEM((HALVES, n_rows, BS, LANES), BF16),
            pltpu.VMEM((HALVES, n_rows, BS, LANES), BF16),
            f32(HALVES, nq, 2, split, step, LANES),
            f32(HALVES, nq, split, step, LANES),
            f32(HALVES, nq, split, step, LANES),
            f32(HALVES, nq - 1, split, step, LANES),
            f32(HALVES, split, step, LANES),
            f32(HALVES, ng, step, LANES),
            f32(HALVES, nq, 2, split, step, LANES),
            *sems(1, HALVES), *sems(2, GROUPS), *sems(1, HALVES, 2), *sems(2, HALVES), *sems(6, HALVES, CHUNKS),
            *sems(2, HALVES), *sems(2, HALVES, nq - 1), *sems(4, HALVES, ng - 1),
            *sems(2, HALVES, nq - 1), *sems(2, HALVES),
        ],
        compiler_params=pltpu.CompilerParams(
            collective_id=0, has_side_effects=True, vmem_limit_bytes=60 * 1024 * 1024
        ),
    )(col_index, live_counts, basis.reshape(n_rows, BS, width), stiffness, mass)
    stiff, massb, kgram, mgram = pl.pallas_call(
        copy_kernel,
        out_shape=(sb, sb, gram, gram),
        in_specs=[hbm] * 4,
        out_specs=(hbm,) * 4,
        scratch_shapes=[sem((4,))],
    )(*outs)
    return (stiff.reshape(n_rows * BS, width), massb.reshape(n_rows * BS, width), kgram, mgram)


def solution(mesh):
    in_specs = (
        P(("loop", "grp"), None),
        P(("loop", "grp"), None, None),
        P(("loop", "grp"), None, None),
        P(("loop", "grp"), None),
        P(("loop", "grp")),
    )
    out_specs = (P(("loop", "grp"), None), P(("loop", "grp"), None), P(), P())
    return jax.shard_map(
        on_device, mesh=mesh, in_specs=in_specs, out_specs=out_specs, check_vma=False
    )
```

time: 54.5 us -> 89.2 us (1.64)
  Pallas kernels: 45.5 us -> 88.3 us
  local copies, waits for them, and re-layouts: 8.05 us -> 0 us
    pallas_call x0 -> x1, Pallas kernels: none -> 40.8 us  [on_device(): pl.pallas_call(copy_kernel, out_shape=(sb, sb, gram, gram), in_specs=[hbm...]
    unnamed x14 -> x0, local copies, waits for them, and re-layouts: 8.05 us -> none
    pallas_call x1, Pallas kernels: 45.5 us -> 47.5 us  [on_device(): pl.pallas_call(functools.partial(fused_kernel, nl, ng, split, factor), ou...]
where the time goes in v3:
time: 89.2 us; the launch traced here: 89 us
  Pallas kernels  88.3 us (99%)
    pallas_call x1, Pallas kernels, on_device(): pl.pallas_call(functools.partial(fused_kernel, nl, ng, split, factor), ou...  47.5 us
    pallas_call x1, Pallas kernels, on_device(): pl.pallas_call(copy_kernel, out_shape=(sb, sb, gram, gram), in_specs=[hbm...  40.8 us

profile of v3, /device:TPU:0, one launch (start us, length us, event | category | flops | bytes accessed | tf_op | source)
XLA Modules:
  0.0 89.0 jit_solution(17350101814025566770)
XLA Ops:
  0.6 47.5 %shard_map.84 = (bf16[12,64,256]{2,1,0:T(8,128)(2,1)}, bf16[12,64,256]{2,1,0:T(8,128)(2,1)}, f32[256,256]{1,0:T(8,128)}, f32[256,256]{1,0:T(8,128)}) custom-call(s32[12,16]{1,0:T(8,128)} %col.1, s32[12]{0:T(128)} %live.1, bf16[12,64,256]{2,1,0:T(8,128)(2,1)} %bitcast.3, bf16[12,16,4096]{2,1,0:T(8,128)(2,1)} %k_hbm.1, bf16[12,16,4096]{2,1,0:T(8,128)(2,1)} %m_hbm.1), custom_call_target="tpu_custom_call" | custom-call | tf_op jit(solution)/shard_map/pallas_call | solution.py:300
  48.1 40.8 %shard_map.85 = (bf16[12,64,256]{2,1,0:T(8,128)(2,1)}, bf16[12,64,256]{2,1,0:T(8,128)(2,1)}, f32[256,256]{1,0:T(8,128)}, f32[256,256]{1,0:T(8,128)}) custom-call(bf16[12,64,256]{2,1,0:T(8,128)(2,1)} %get-tuple-element.12.refs_0_, bf16[12,64,256]{2,1,0:T(8,128)(2,1)} %get-tuple-element.13.refs_1_, f32[256,256]{1,0:T(8,128)} %get-tuple-element.14.refs_2_, ...), custom_call_target="tpu_custom_call" | custom-call | tf_op jit(solution)/shard_map/pallas_call | solution.py:334

commit v4 on v2

--- a/solution.py
+++ b/solution.py
@@ -168,25 +168,37 @@
     c.start()
     c.wait()
     half[...] = part[:, me_c] + land_c[...]
-    copies = [
-        send(half.at[lax.rem(me_q + d, nq)], land_q.at[d - 1], s_a2.at[d - 1], r_a2.at[d - 1], chip(d))
-        for d in range(1, nq)
+    whole = split == 1
+    chips = [
+        [
+            send(
+                half.at[lax.rem(me_q + d, nq), g], land_q.at[d - 1, g], s_a2.at[d - 1, i], r_a2.at[d - 1, i], chip(d))
+            for d in range(1, nq)
+        ]
+        for i in range(split)
+        for g in [lax.rem(me_g + 1 + i, split)]
     ]
-    for c in copies:
-        c.start()
-    for c in copies:
-        c.wait()
-    total = half[me_q]
-    for d in range(1, nq):
-        total = total + land_q[d - 1]
-    red[...] = total
-    whole = split == 1
-    copies = [
-        send(red.at[0] if whole else red.at[lax.rem(me_g + d, ng)], land_g.at[d - 1], s_b.at[d - 1], r_b.at[d - 1], grp(d))
-        for d in range(1, ng)
-    ]
-    for c in copies:
-        c.start()
+    for pair in chips:
+        for c in pair:
+            c.start()
+    copies = []
+    for i in range(split):
+        g = lax.rem(me_g + 1 + i, split)
+        total = half[me_q, g]
+        for d in range(1, nq):
+            chips[i][d - 1].wait_recv()
+            total = total + land_q[d - 1, g]
+        red[g] = total
+        if not whole and i < ng - 1:
+            copies.append(send(red.at[g], land_g.at[i], s_b.at[i], r_b.at[i], grp(i + 1)))
+            copies[-1].start()
+    if whole:
+        copies = [send(red.at[0], land_g.at[d - 1], s_b.at[d - 1], r_b.at[d - 1], grp(d)) for d in range(1, ng)]
+        for c in copies:
+            c.start()
+    for pair in chips:
+        for c in pair:
+            c.wait_send()
     for c in copies:
         c.wait()
     if whole:
@@ -201,15 +213,20 @@
             mine = mine + land_g[d - 1]
         res[me_q, me_c, me_g] = mine * factor
         piece = res.at[me_q, me_c, me_g]
-        copies = [send(piece, piece, s_c.at[d - 1], r_c.at[d - 1], grp(d)) for d in range(1, ng)]
-        for c in copies:
-            c.start()
-        for c in copies:
-            c.wait()
-    piece = res.at[me_q, me_c]
-    copies = [send(piece, piece, s_d1.at[d - 1], r_d1.at[d - 1], chip(d)) for d in range(1, nq)]
-    for c in copies:
-        c.start()
+        gather = [send(piece, piece, s_c.at[d - 1], r_c.at[d - 1], grp(d)) for d in range(1, ng)]
+        for c in gather:
+            c.start()
+    copies = []
+    for i in range(split):
+        if i > 0:
+            gather[i - 1].wait_recv()
+        piece = res.at[me_q, me_c, lax.rem(me_g + split - i, split)]
+        for d in range(1, nq):
+            copies.append(send(piece, piece, s_d1.at[d - 1, i], r_d1.at[d - 1, i], chip(d)))
+            copies[-1].start()
+    if not whole:
+        for c in gather:
+            c.wait_send()
     for c in copies:
         c.wait()
     piece = res.at[:, me_c]
@@ -220,6 +237,15 @@
         for i in range(pieces):
             n = m * pieces + i
             dst[i * step : (i + 1) * step, :] = res[n // (2 * split), n // split % 2, n % split]
+
+
+def copy_kernel(*refs):
+    n = len(refs) // 2
+    copies = [pltpu.make_async_copy(refs[i], refs[n + i], refs[-1].at[i]) for i in range(n)]
+    for c in copies:
+        c.start()
+    for c in copies:
+        c.wait()
 
 
 def on_device(basis, stiffness, mass, col_index, live_counts):
@@ -235,7 +261,7 @@
     sem = pltpu.SemaphoreType.DMA
     sb = jax.ShapeDtypeStruct((n_rows, BS, width), BF16)
     gram = jax.ShapeDtypeStruct((width, width), F32)
-    stiff, massb, kgram, mgram = pl.pallas_call(
+    outs = pl.pallas_call(
         functools.partial(fused_kernel, nl, ng, split, factor),
         out_shape=(sb, sb, gram, gram),
         in_specs=[smem, smem, hbm, hbm, hbm],
@@ -260,14 +286,21 @@
             pltpu.VMEM((nq, 2, split, step, width), F32),
             sem(()), sem((GROUPS,)), sem((GROUPS,)), sem(()), sem(()),
             sem((GROUPS,)), sem((GROUPS,)), sem((GROUPS,)), sem((GROUPS,)), sem((GROUPS,)), sem((GROUPS,)),
-            sem(()), sem(()), sem((nq - 1,)), sem((nq - 1,)),
+            sem(()), sem(()), sem((nq - 1, split)), sem((nq - 1, split)),
             sem((ng - 1,)), sem((ng - 1,)), sem((ng - 1,)), sem((ng - 1,)),
-            sem((nq - 1,)), sem((nq - 1,)), sem(()), sem(()),
+            sem((nq - 1, split)), sem((nq - 1, split)), sem(()), sem(()),
         ],
         compiler_params=pltpu.CompilerParams(
-            collective_id=0, has_side_effects=True, vmem_limit_bytes=40 * 1024 * 1024
+            collective_id=0, has_side_effects=True, vmem_limit_bytes=60 * 1024 * 1024
         ),
     )(col_index, live_counts, basis.reshape(n_rows, BS, width), stiffness, mass)
+    stiff, massb, kgram, mgram = pl.pallas_call(
+        copy_kernel,
+        out_shape=(sb, sb, gram, gram),
+        in_specs=[vmem] * 4,
+        out_specs=(hbm,) * 4,
+        scratch_shapes=[sem((4,))],
+    )(*outs)
     return (stiff.reshape(n_rows * BS, width), massb.reshape(n_rows * BS, width), kgram, mgram)
 
 

time: 54.5 us -> 47.4 us (0.87)
  local copies, waits for them, and re-layouts: 8.05 us -> 0 us
  Pallas kernels: 45.5 us -> 46.6 us
    unnamed x14 -> x0, local copies, waits for them, and re-layouts: 8.05 us -> none
    pallas_call x0 -> x1, Pallas kernels: none -> 2.35 us  [on_device(): pl.pallas_call(copy_kernel, out_shape=(sb, sb, gram, gram), in_specs=[vme...]
    pallas_call x1, Pallas kernels: 45.5 us -> 44.2 us  [on_device(): pl.pallas_call(functools.partial(fused_kernel, nl, ng, split, factor), ou...]
where the time goes in v4:
time: 47.4 us; the launch traced here: 47.2 us
  Pallas kernels  46.6 us (98%)
  between operations  0.64 us (1%)
    pallas_call x1, Pallas kernels, on_device(): pl.pallas_call(functools.partial(fused_kernel, nl, ng, split, factor), ou...  44.2 us
    pallas_call x1, Pallas kernels, on_device(): pl.pallas_call(copy_kernel, out_shape=(sb, sb, gram, gram), in_specs=[vme...  2.35 us

profile of v4, /device:TPU:0, one launch (start us, length us, event | category | flops | bytes accessed | tf_op | source)
XLA Modules:
  0.0 47.2 jit_solution(15591810820746725315)
XLA Ops:
  0.6 44.2 %shard_map.84 = (bf16[12,64,256]{2,1,0:T(8,128)(2,1)}, bf16[12,64,256]{2,1,0:T(8,128)(2,1)}, f32[256,256]{1,0:T(8,128)}, f32[256,256]{1,0:T(8,128)}) custom-call(s32[12,16]{1,0:T(8,128)} %col.1, s32[12]{0:T(128)} %live.1, bf16[12,64,256]{2,1,0:T(8,128)(2,1)} %bitcast.3, bf16[12,16,4096]{2,1,0:T(8,128)(2,1)} %k_hbm.1, bf16[12,16,4096]{2,1,0:T(8,128)(2,1)} %m_hbm.1), custom_call_target="tpu_custom_call" | custom-call | tf_op jit(solution)/shard_map/pallas_call | solution.py:264
  44.9 2.3 %shard_map.85 = (bf16[12,64,256]{2,1,0:T(8,128)(2,1)}, bf16[12,64,256]{2,1,0:T(8,128)(2,1)}, f32[256,256]{1,0:T(8,128)}, f32[256,256]{1,0:T(8,128)}) custom-call(bf16[12,64,256]{2,1,0:T(8,128)(2,1)} %get-tuple-element.12.refs_0_, bf16[12,64,256]{2,1,0:T(8,128)(2,1)} %get-tuple-element.13.refs_1_, f32[256,256]{1,0:T(8,128)} %get-tuple-element.14.refs_2_, ...), custom_call_target="tpu_custom_call" | custom-call | tf_op jit(solution)/shard_map/pallas_call | solution.py:297

commit v5 on v4

--- a/solution.py
+++ b/solution.py
@@ -206,12 +206,12 @@
         mine = land_g[lax.rem(me_g + ng - 1, ng)]
         for g in range(1, ng):
             mine = mine + land_g[lax.rem(me_g - g + 2 * ng - 1, ng)]
-        res[me_q, me_c, 0] = mine * factor
+        res[me_q, me_c, 0] = (mine * factor).astype(BF16)
     else:
         mine = red[me_g]
         for d in range(1, ng):
             mine = mine + land_g[d - 1]
-        res[me_q, me_c, me_g] = mine * factor
+        res[me_q, me_c, me_g] = (mine * factor).astype(BF16)
         piece = res.at[me_q, me_c, me_g]
         gather = [send(piece, piece, s_c.at[d - 1], r_c.at[d - 1], grp(d)) for d in range(1, ng)]
         for c in gather:
@@ -236,7 +236,7 @@
     for m, dst in enumerate((kgram, mgram)):
         for i in range(pieces):
             n = m * pieces + i
-            dst[i * step : (i + 1) * step, :] = res[n // (2 * split), n // split % 2, n % split]
+            dst[i * step : (i + 1) * step, :] = res[n // (2 * split), n // split % 2, n % split].astype(F32)
 
 
 def copy_kernel(*refs):
@@ -283,7 +283,7 @@
             pltpu.VMEM((nq - 1, split, step, width), F32),
             pltpu.VMEM((split, step, width), F32),
             pltpu.VMEM((ng, step, width), F32),
-            pltpu.VMEM((nq, 2, split, step, width), F32),
+            pltpu.VMEM((nq, 2, split, step, width), BF16),
             sem(()), sem((GROUPS,)), sem((GROUPS,)), sem(()), sem(()),
             sem((GROUPS,)), sem((GROUPS,)), sem((GROUPS,)), sem((GROUPS,)), sem((GROUPS,)), sem((GROUPS,)),
             sem(()), sem(()), sem((nq - 1, split)), sem((nq - 1, split)),

time: 47.4 us -> 46.4 us (0.979)
  Pallas kernels: 46.6 us -> 45.5 us
    pallas_call x1, Pallas kernels: 44.2 us -> 43.2 us  [on_device(): pl.pallas_call(functools.partial(fused_kernel, nl, ng, split, factor), ou...]
where the time goes in v5:
time: 46.4 us; the launch traced here: 46.2 us
  Pallas kernels  45.5 us (98%)
  between operations  0.64 us (1%)
    pallas_call x1, Pallas kernels, on_device(): pl.pallas_call(functools.partial(fused_kernel, nl, ng, split, factor), ou...  43.2 us
    pallas_call x1, Pallas kernels, on_device(): pl.pallas_call(copy_kernel, out_shape=(sb, sb, gram, gram), in_specs=[vme...  2.35 us

profile of v5, /device:TPU:0, one launch (start us, length us, event | category | flops | bytes accessed | tf_op | source)
XLA Modules:
  0.0 46.2 jit_solution(14168465978070755688)
XLA Ops:
  0.6 43.2 %shard_map.84 = (bf16[12,64,256]{2,1,0:T(8,128)(2,1)}, bf16[12,64,256]{2,1,0:T(8,128)(2,1)}, f32[256,256]{1,0:T(8,128)}, f32[256,256]{1,0:T(8,128)}) custom-call(s32[12,16]{1,0:T(8,128)} %col.1, s32[12]{0:T(128)} %live.1, bf16[12,64,256]{2,1,0:T(8,128)(2,1)} %bitcast.3, bf16[12,16,4096]{2,1,0:T(8,128)(2,1)} %k_hbm.1, bf16[12,16,4096]{2,1,0:T(8,128)(2,1)} %m_hbm.1), custom_call_target="tpu_custom_call" | custom-call | tf_op jit(solution)/shard_map/pallas_call | solution.py:264
  43.8 2.3 %shard_map.85 = (bf16[12,64,256]{2,1,0:T(8,128)(2,1)}, bf16[12,64,256]{2,1,0:T(8,128)(2,1)}, f32[256,256]{1,0:T(8,128)}, f32[256,256]{1,0:T(8,128)}) custom-call(bf16[12,64,256]{2,1,0:T(8,128)(2,1)} %get-tuple-element.12.refs_0_, bf16[12,64,256]{2,1,0:T(8,128)(2,1)} %get-tuple-element.13.refs_1_, f32[256,256]{1,0:T(8,128)} %get-tuple-element.14.refs_2_, ...), custom_call_target="tpu_custom_call" | custom-call | tf_op jit(solution)/shard_map/pallas_call | solution.py:297
